TPU v7x, 256 devices: a whole 4x4x8 slice. The times are simulated.
256 devices in a mesh: req: 64 (over x, z, core), tensor: 4 (over y).
Axes of the slice: x: 4, y: 4, z: 8, core: 2. Of those that a mesh axis runs over, the one named last changes fastest.
Arguments:
- stream: bfloat16 [65536, 2048], P('req', 'tensor'), may hold values from -64 to 64
- target_row: int32 [65536], P('req'), may hold values from -1 to 65535, as said below
- segment_ids: int32 [65536], P('req'), may hold values from -1 to 63, as said below
- cache_slot: int32 [65536], P('req'), may hold values from -1 to 2047, as said below
- norm_gain: bfloat16 [2048], replicated, may hold values from 0.099609375 to 1.8984375
- norm_bias: bfloat16 [2048], replicated, may hold values from -3 to 3
- projection: bfloat16 [2048, 3, 2048], P(None, None, 'tensor'), may hold values from -1 to 1
- output_weight: bfloat16 [2048, 2048], P('tensor'), may hold values from -0.125 to 0.125
- cache_pool: bfloat16 [131072, 2, 2048], P('req', None, 'tensor'), may hold values from -6 to 6
Outputs:
- mixed: bfloat16 [65536, 2048], P('req', 'tensor')
- new_pool: bfloat16 [131072, 2, 2048], P('req', None, 'tensor')
Inputs may be any that keep to these rules, and one draw needn't show every extreme that they name: `target_row`: every live row of the request layout is named by exactly one stream row and no other row is named. A device names at most 16 rows of any one device; in every draw some device receives exactly 16 rows from every device and its 1024 rows are all live. `segment_ids`: within one device's 1024 rows the numbers start at 0 on the first row, rise by one at each new request and never fall; a request's rows are consecutive and never cross devices; -1 only on the rows after the last request. A device holds at most 64 requests, and in every draw some device holds exactly that many. `cache_slot`: live rows of one device have distinct slots; a request's rows fill its pages in order, each page being 16 consecutive slots beginning at a multiple of 16; -1 exactly on rows where segment_ids is -1.
All inputs are finite; a program needn't handle non-finite values.
Results may differ from a plain program's by a relative error of at most 0.008.
Values may be sent and summed in bfloat16 or wider, within the bound.
No kernel may reach another device: no remote copies, remote signals or barrier semaphores. Data moves between devices by JAX's collectives and lax.ppermute only.
A program may use at most 128 MiB of HBM per device.

v0:
```python
import functools
import math

import jax
import jax.numpy as jnp
from jax import lax
from jax.experimental import pallas as pl
from jax.experimental.pallas import tpu as pltpu
from jax.sharding import PartitionSpec as P

HDIM = 256
ROT = 64
LANES = 128
CHUNKS = 2

norm_epsilon = 1e-05
masked_score = -1e30
rotary_base = 10000.0

bf16 = jnp.bfloat16
f32 = jnp.float32
i32 = jnp.int32


def iota(shape, dim):
    return lax.broadcasted_iota(i32, shape, dim)


def hot(condition):
    return jnp.where(condition, 1.0, 0.0).astype(bf16)


def dot(a, b):
    return jnp.dot(a, b, preferred_element_type=f32)


def dot_nt(a, b):
    return lax.dot_general(a, b, (((1,), (1,)), ((), ())), preferred_element_type=f32)


def whole(shape):
    zeros = (0,) * len(shape)
    return pl.BlockSpec(shape, lambda *_: zeros)


def pack_kernel(target_ref, stream_ref, packed_ref, *, peers):
    row_count = target_ref.shape[1]
    cap = row_count // peers
    width = stream_ref.shape[1]
    parts = width // LANES
    target = target_ref[...]
    sends = target >= 0
    receiver = jnp.where(sends, target // row_count, peers)
    local = jnp.where(sends, target - receiver * row_count + 1, 0)
    onehot = jnp.where(iota((peers, row_count), 0) == receiver, 1.0, 0.0)
    upper = hot(iota((LANES, LANES), 0) < iota((LANES, LANES), 1))
    carry = jnp.zeros((peers, 1), f32)
    ranks = []
    for start in range(0, row_count, LANES):
        block = onehot[:, start : start + LANES]
        before = dot(block.astype(bf16), upper) + carry
        ranks.append(jnp.sum(block * before, axis=0, keepdims=True))
        carry = carry + jnp.sum(block, axis=1, keepdims=True)
    rank = jnp.concatenate(ranks, axis=1).astype(i32)
    slot = jnp.where(sends, receiver * cap + rank, -1)
    high = local // 32
    low = local - high * 32
    lane = iota((LANES, row_count), 0)
    table = dot_nt((onehot * high.astype(f32)).astype(bf16), hot(lane == rank)) + dot_nt(
        (onehot * low.astype(f32)).astype(bf16), hot(lane == rank + cap)
    )
    repeat = hot(iota((peers * 8, peers), 0) // 8 == iota((peers * 8, peers), 1))
    packed_ref[:, cap * parts :, :] = (
        dot(repeat, table.astype(bf16)).reshape(peers, 8, LANES).astype(bf16)
    )
    step = 256
    for start in range(0, row_count, step):
        chosen = hot(iota((step, row_count), 0) + start == slot)
        rows = dot(chosen, stream_ref[...])
        first = start // cap
        for part in range(parts):
            packed_ref[first : first + step // cap, part * cap : (part + 1) * cap, :] = (
                rows[:, part * LANES : (part + 1) * LANES].reshape(step // cap, cap, LANES).astype(bf16)
            )


def pack(target, stream, peers):
    row_count, width = stream.shape
    cap = row_count // peers
    return pl.pallas_call(
        functools.partial(pack_kernel, peers=peers),
        out_shape=jax.ShapeDtypeStruct((peers, cap * (width // LANES) + 8, LANES), bf16),
        name="pack",
    )(target.reshape(1, row_count), stream)


def unpack_kernel(got_ref, *placed_refs):
    peers = got_ref.shape[0]
    chunk, width = placed_refs[0].shape
    row_count = chunk * len(placed_refs)
    cap = row_count // peers
    parts = width // LANES
    tables = got_ref[:, cap * parts :, :].astype(f32).reshape(peers * 8, LANES).astype(bf16)
    table = dot(hot(iota((peers, peers * 8), 1) == 8 * iota((peers, peers * 8), 0)), tables)
    table = table.astype(bf16)
    lane = iota((LANES, row_count), 0)
    rank = iota((LANES, row_count), 1) % cap
    value = 32.0 * dot(table, hot(lane == rank)) + dot(table, hot(lane == rank + cap))
    owner = iota((peers, row_count), 1) // cap == iota((peers, row_count), 0)
    arrived = jnp.sum(jnp.where(owner, value, 0.0), axis=0, keepdims=True).astype(i32) - 1
    for number, placed_ref in enumerate(placed_refs):
        chosen = hot(iota((chunk, row_count), 0) + number * chunk == arrived)
        for part in range(parts):
            rows = got_ref[:, part * cap : (part + 1) * cap, :].reshape(row_count, LANES)
            placed_ref[:, part * LANES : (part + 1) * LANES] = dot(chosen, rows).astype(bf16)


def unpack(got, row_count, width):
    chunk = row_count // CHUNKS
    return pl.pallas_call(
        unpack_kernel,
        out_shape=[jax.ShapeDtypeStruct((chunk, width), bf16)] * CHUNKS,
        name="unpack",
    )(got)


def layer_kernel(number, group_ref, *refs):
    own, left, right, far_top, far_bottom, *weights = refs[:8]
    gain, bias, cosine, sine, segment_row, segment_col = refs[8:14]
    rest = refs[14:]
    past_keys, past_values, (context, keys_out, values_out) = (
        rest[:number],
        rest[number : 2 * number],
        rest[2 * number :],
    )
    chunk, width = own.shape
    groups = gain.shape[1] // width
    me = group_ref[0]
    pieces = [
        own[...].astype(f32),
        left[...].astype(f32),
        jnp.concatenate([far_top[...], far_bottom[...]], axis=0).astype(f32),
        right[...].astype(f32),
    ]
    total = sum(jnp.sum(piece, axis=1, keepdims=True) for piece in pieces)
    mean = total * (1.0 / (width * groups))
    centred = [piece - mean for piece in pieces]
    spread = sum(jnp.sum(piece * piece, axis=1, keepdims=True) for piece in centred)
    scale = lax.rsqrt(spread * (1.0 / (width * groups)) + norm_epsilon)
    projected = [0.0, 0.0, 0.0]
    for offset, piece in enumerate(centred):
        source = lax.rem(me + groups - offset, groups)
        place = pl.ds(pl.multiple_of(source * width, width), width)
        normed = (piece * scale * gain[:, place].astype(f32) + bias[:, place].astype(f32)).astype(bf16)
        projected = [total + dot(normed, weight[place, :]) for total, weight in zip(projected, weights)]
    raw_queries, raw_keys, raw_values = [total.astype(bf16) for total in projected]
    cos_part = cosine[...]
    sin_part = sine[...]
    even = iota((chunk, LANES), 1) % 2 == 0

    def turn(head):
        lead = head[:, :LANES].astype(f32)
        swapped = jnp.where(even, pltpu.roll(lead, LANES - 1, 1), pltpu.roll(lead, 1, 1))
        turned = (lead * cos_part + swapped * sin_part).astype(bf16)
        return jnp.concatenate([turned, head[:, LANES:]], axis=1)

    segment = segment_col[...]
    allowed = []
    for block in range(number + 1):
        same = segment_row[:, block * chunk : (block + 1) * chunk] == segment
        if block == number:
            same = same & (iota((chunk, chunk), 1) <= iota((chunk, chunk), 0))
        allowed.append(same)
    score_scale = 1.0 / math.sqrt(HDIM)
    for head in range(width // HDIM):
        cols = slice(head * HDIM, (head + 1) * HDIM)
        query = turn(raw_queries[:, cols])
        key = turn(raw_keys[:, cols])
        value = raw_values[:, cols]
        keys_out[:, cols] = key
        values_out[:, cols] = value
        keys = [ref[:, cols] for ref in past_keys] + [key]
        values = [ref[:, cols] for ref in past_values] + [value]
        scores = [
            jnp.where(mask, dot_nt(query, block) * score_scale, masked_score)
            for mask, block in zip(allowed, keys)
        ]
        top = functools.reduce(jnp.maximum, [jnp.max(s, axis=1, keepdims=True) for s in scores])
        raised = [jnp.where(mask, jnp.exp(s - top), 0.0) for mask, s in zip(allowed, scores)]
        row_total = sum(jnp.sum(r, axis=1, keepdims=True) for r in raised)
        inverse = 1.0 / row_total
        mixed = sum(dot((r * inverse).astype(bf16), v) for r, v in zip(raised, values))
        context[:, cols] = mixed.astype(bf16)


def layer(number, group, pieces, weights, gain, bias, cosine, sine, segment_row, segment_col, keys, values):
    chunk, width = pieces[0].shape
    by_chunk = lambda columns: pl.BlockSpec((chunk, columns), lambda i, g: (number, 0))
    rows = jax.ShapeDtypeStruct((chunk, width), bf16)
    return pl.pallas_call(
        functools.partial(layer_kernel, number),
        grid_spec=pltpu.PrefetchScalarGridSpec(
            num_scalar_prefetch=1,
            grid=(1,),
            in_specs=[whole(piece.shape) for piece in pieces]
            + [whole(array.shape) for array in (*weights, gain, bias)]
            + [by_chunk(LANES), by_chunk(LANES), whole(segment_row.shape), by_chunk(1)]
            + [whole(rows.shape)] * (2 * number),
            out_specs=[whole(rows.shape)] * 3,
        ),
        out_shape=[rows] * 3,
        compiler_params=pltpu.CompilerParams(vmem_limit_bytes=40 << 20),
        name="layer",
    )(group, *pieces, *weights, gain, bias, cosine, sine, segment_row, segment_col, *keys, *values)


def finish_kernel(*refs):
    own, left, right, far_top, far_bottom, w_own, w_left, w_far, w_right, placed, segment_col = refs[:11]
    mixed = refs[-1]
    total = dot(own[...], w_own[...]) + dot(left[...], w_left[...]) + dot(right[...], w_right[...])
    total = total + dot(jnp.concatenate([far_top[...], far_bottom[...]], axis=0), w_far[...])
    mixed[...] = jnp.where(segment_col[...] >= 0, placed[...].astype(f32) + total, 0.0).astype(bf16)


def finish(number, pieces, weights, placed, segment_col, buffer):
    chunk, width = placed.shape
    row_count = segment_col.shape[0]
    given = [*pieces, *weights, placed]
    specs = [whole(array.shape) for array in given] + [pl.BlockSpec((chunk, 1), lambda i: (number, 0))]
    given.append(segment_col)
    aliases = {}
    if buffer is not None:
        aliases = {len(given): 0}
        given.append(buffer)
        specs.append(pl.BlockSpec(memory_space=pl.ANY))
    return pl.pallas_call(
        finish_kernel,
        grid=(1,),
        in_specs=specs,
        out_specs=pl.BlockSpec((chunk, width), lambda i: (number, 0)),
        out_shape=jax.ShapeDtypeStruct((row_count, width), bf16),
        input_output_aliases=aliases,
        compiler_params=pltpu.CompilerParams(vmem_limit_bytes=16 << 20),
        name="finish",
    )(*given)


def pool_kernel(slot_ref, old_ref, *refs):
    *row_refs, out_ref, spread_ref = refs
    row_count = slot_ref.shape[1]
    half = len(row_refs) // 2
    width = row_refs[0].shape[1]
    parts = width // LANES
    chunk = row_refs[0].shape[0]
    per_slot = 2 * parts
    step = out_ref.shape[0] // per_slot
    chosen = hot(iota((step, row_count), 0) + pl.program_id(0) * step == slot_ref[...])
    found = jnp.sum(chosen.astype(f32), axis=1, keepdims=True)
    for which in range(2):
        rows = sum(
            dot(chosen[:, number * chunk : (number + 1) * chunk], ref[...])
            for number, ref in enumerate(row_refs[which * half : (which + 1) * half])
        )
        for part in range(parts):
            spread_ref[pl.ds(2 * part + which, step, stride=per_slot), :] = rows[
                :, part * LANES : (part + 1) * LANES
            ]
    repeat = hot(iota((step * per_slot, step), 0) // per_slot == iota((step * per_slot, step), 1))
    written = dot(repeat, jnp.broadcast_to(found, (step, LANES)).astype(bf16))
    out_ref[...] = jnp.where(written > 0.5, spread_ref[...].astype(bf16), old_ref[...])


def write_pool(live_slot, cache_pool, keys, values):
    slots, pair, width = cache_pool.shape
    parts = width // LANES
    per_slot = pair * parts
    step = 256
    row_count = live_slot.shape[0]
    flat = cache_pool.reshape(slots, pair, parts, LANES).transpose(0, 2, 1, 3).reshape(slots * per_slot, LANES)
    block = pl.BlockSpec((step * per_slot, LANES), lambda i: (i, 0))
    rows = [*keys, *values]
    out = pl.pallas_call(
        pool_kernel,
        grid=(slots // step,),
        in_specs=[whole((1, row_count)), block] + [whole(array.shape) for array in rows],
        out_specs=block,
        out_shape=jax.ShapeDtypeStruct(flat.shape, bf16),
        scratch_shapes=[pltpu.VMEM((step * per_slot, LANES), f32)],
        compiler_params=pltpu.CompilerParams(vmem_limit_bytes=32 << 20),
        name="pool",
    )(live_slot.reshape(1, row_count), flat, *rows)
    return out.reshape(slots, parts, pair, LANES).transpose(0, 2, 1, 3).reshape(slots, pair, width)


def shift(values, distance):
    size = lax.axis_size("tensor")
    return lax.ppermute(values, "tensor", [(i, (i + distance) % size) for i in range(size)])


def gather_pieces(own):
    half = own.shape[0] // 2
    left = shift(own, 1)
    right = shift(own, -1)
    return own, left, right, shift(left[:half], 1), shift(right[half:], -1)


def rotary_tables(segment_ids):
    row_count = segment_ids.shape[0]
    row_ids = jnp.arange(row_count, dtype=i32)
    earlier = (segment_ids[:, None] == segment_ids[None, :]) & (row_ids[None, :] < row_ids[:, None])
    position = jnp.sum(earlier.astype(i32), axis=1)
    lane = jnp.arange(LANES, dtype=i32)
    exponent = (lane // 2).astype(f32) * (2.0 / ROT)
    inverse_freq = 1.0 / rotary_base**exponent
    angles = position.astype(f32)[:, None] * inverse_freq[None, :]
    turned = (lane < ROT)[None, :]
    sign = jnp.where(lane % 2 == 0, -1.0, 1.0)[None, :]
    return jnp.where(turned, jnp.cos(angles), 1.0), jnp.where(turned, jnp.sin(angles) * sign, 0.0)


def shards(
    stream,
    target_row,
    segment_ids,
    cache_slot,
    norm_gain,
    norm_bias,
    projection,
    output_weight,
    cache_pool,
):
    peers = lax.axis_size("req")
    groups = lax.axis_size("tensor")
    me = lax.axis_index("tensor")
    row_count, width = stream.shape
    depth = projection.shape[0]

    packed = pack(target_row, stream, peers)
    packed, projection, output_weight, segment_ids, cache_slot = lax.optimization_barrier(
        (packed, projection, output_weight, segment_ids, cache_slot)
    )
    got = lax.all_to_all(packed, "req", split_axis=0, concat_axis=0, tiled=True)

    weights = [projection[:, which, :] for which in range(3)]
    cosine, sine = rotary_tables(segment_ids)
    segment_row = segment_ids.reshape(1, row_count)
    segment_col = segment_ids.reshape(row_count, 1)
    live_slot = jnp.where(segment_ids >= 0, cache_slot, -1)
    gain = norm_gain.reshape(1, depth)
    bias = norm_bias.reshape(1, depth)
    out_weights = []
    for offset in range(groups):
        target = lax.rem(me + offset, groups)
        block = lax.dynamic_slice_in_dim(output_weight, target * width, width, axis=1)
        out_weights.append(block if offset == 0 else shift(block, offset))
    group = me.astype(i32).reshape(1)
    got, weights, cosine, sine, segment_col, out_weights = lax.optimization_barrier(
        (got, weights, cosine, sine, segment_col, out_weights)
    )

    placed = unpack(got, row_count, width)
    gathered = []
    for chunk in placed:
        if gathered:
            chunk, _ = lax.optimization_barrier((chunk, gathered[-1][1:3]))
        gathered.append(gather_pieces(chunk))
    keys, values, contexts = [], [], []
    for number in range(CHUNKS):
        context, key, value = layer(
            number, group, gathered[number], weights, gain, bias, cosine, sine, segment_row, segment_col, keys, values
        )
        keys.append(key)
        values.append(value)
        contexts.append(gather_pieces(context))
    mixed = None
    for number in range(CHUNKS):
        mixed = finish(number, contexts[number], out_weights, placed[number], segment_col, mixed)
    return (mixed, write_pool(live_slot, cache_pool, keys, values))


def solution(mesh):
    in_specs = (
        P("req", "tensor"),
        P("req"),
        P("req"),
        P("req"),
        P(),
        P(),
        P(None, None, "tensor"),
        P("tensor", None),
        P("req", None, "tensor"),
    )
    out_specs = (P("req", "tensor"), P("req", None, "tensor"))
    return jax.shard_map(shards, mesh=mesh, in_specs=in_specs, out_specs=out_specs, check_vma=False)
```

profile of v0, /device:TPU:2, one launch (start us, length us, event | category | flops | bytes accessed | tf_op | source)
XLA Modules:
  0.0 152.9 jit_solution(17438142466427938664)
XLA Ops:
  0.6 4.4 %pack.1 = bf16[64,72,128]{2,1,0:T(8,128)(2,1)} custom-call(s32[1,1024]{1,0:T(1,128)} %bitcast.27, bf16[1024,512]{1,0:T(8,128)(2,1)} %stream_ref.1), custom_call_target="tpu_custom_call" | custom-call | tf_op jit(solution)/shard_map/pack/pallas_call | solution.py:90
  5.1 12.2 %all-to-all-start = ((bf16[64,72,128]{2,1,0:T(8,128)(2,1)}), bf16[64,72,128]{2,1,0:T(8,128)(2,1)}, u32[]{:S(2)}, u32[]{:S(2)}) async-start(bf16[64,72,128]{2,1,0:T(8,128)(2,1)} %pack.1), calls=%async_computation | async-start | bytes 2359296 | tf_op jit(solution)/shard_map/all_to_all | solution.py:342
  17.3 0.0 copy-start.24
  17.3 0.2 constant_dynamic-slice_fusion
  17.6 1.7 %collective-permute-start = (bf16[512,512]{1,0:T(8,128)(2,1)S(1)}, bf16[512,512]{1,0:T(8,128)(2,1)S(1)}, u32[]{:S(2)}, u32[]{:S(2)}) collective-permute-start(bf16[512,512]{1,0:T(8,128)(2,1)S(1)} %get-tuple-element.57), channel_id=1, source_target_pairs={{0,1},{1,2},{2,3},{3,0},{4,5},{5,6},{6,7},{7,4},{8,9},{9,10},{10,1... | collective-permute-start | bytes 1572872 | tf_op jit(solution)/shard_map/ppermute | solution.py:297
  19.2 2.9 %collective-permute-start.1 = (bf16[512,512]{1,0:T(8,128)(2,1)S(1)}, bf16[512,512]{1,0:T(8,128)(2,1)S(1)}, u32[]{:S(2)}, u32[]{:S(2)}) collective-permute-start(bf16[512,512]{1,0:T(8,128)(2,1)S(1)} %get-tuple-element.56), channel_id=1, source_target_pairs={{0,2},{1,3},{2,0},{3,1},{4,6},{5,7},{6,4},{7,5},{8,10},{9,11},{10,... | collective-permute-start | bytes 1572872 | tf_op jit(solution)/shard_map/ppermute | solution.py:297
  22.1 1.3 collective-permute-start.2
  23.5 0.5 convert_reduce_fusion
  24.1 3.1 %fusion.3 = (f32[1024,128]{1,0:T(8,128)}, f32[1024,128]{1,0:T(8,128)}) fusion(f32[128]{0:T(128)S(1)} %get-tuple-element.61, f32[128]{0:T(128)S(1)} %get-tuple-element.62, f32[1024]{0:T(1024)S(1)} %convert_element_type.18, pred[128]{0:T(512)(128)(4,1)S(1)} %iota_compare_fusion.1), kind=kLoop, calls=%fused_computation.10 | loop fusion | flops 524288 | bytes 1053824 | tf_op jit(solution)/shard_map/jit(_where)/select_n | solution.py:318
  27.2 5.3 %slice_bitcast_fusion = (bf16[2048,512]{1,0:T(8,128)(2,1)S(1)}, bf16[2048,512]{1,0:T(8,128)(2,1)}, bf16[2048,512]{1,0:T(8,128)(2,1)}) fusion(bf16[2048,3,512]{2,0,1:T(8,128)(2,1)} %param.15), kind=kLoop, calls=%fused_computation.3 | loop fusion | bytes 12582912 | tf_op jit(solution)/shard_map/squeeze | solution.py:344
  32.5 0.5 collective-permute-done.refs_6_
  32.9 12.4 %collective-permute-done.1.refs_7_ = bf16[512,512]{1,0:T(8,128)(2,1)S(1)} collective-permute-done((bf16[512,512]{1,0:T(8,128)(2,1)S(1)}, bf16[512,512]{1,0:T(8,128)(2,1)S(1)}, u32[]{:S(2)}, u32[]{:S(2)}) %collective-permute-start.1) | collective-permute-done | bytes 524320 | tf_op jit(solution)/shard_map/ppermute | solution.py:297
  45.3 0.8 copy-done.9
  46.1 0.0 collective-permute-done.2.refs_8_
  46.1 0.8 copy-done.11
  46.9 0.3 all-to-all-done.got_ref
  47.2 4.7 %unpack.1 = (bf16[512,512]{1,0:T(8,128)(2,1)}, bf16[512,512]{1,0:T(8,128)(2,1)}) custom-call(bf16[64,72,128]{2,1,0:T(8,128)(2,1)} %all-to-all-done.got_ref), custom_call_target="tpu_custom_call" | custom-call | tf_op jit(solution)/shard_map/unpack/pallas_call | solution.py:120
  51.9 3.0 %collective-permute-start.4 = (bf16[512,512]{1,0:T(8,128)(2,1)}, bf16[512,512]{1,0:T(8,128)(2,1)S(1)}, u32[]{:S(2)}, u32[]{:S(2)}) collective-permute-start(bf16[512,512]{1,0:T(8,128)(2,1)} %get-tuple-element.33.refs_0_.refs_9_), channel_id=1, source_target_pairs={{0,3},{1,0},{2,1},{3,2},{4,7},{5,4},{6,5},{7,6},{8,11},{9,8},{10,9... | collective-permute-start | bytes 1572872 | tf_op jit(solution)/shard_map/ppermute | solution.py:297
  54.9 0.0 collective-permute-start.3
  54.9 12.4 %collective-permute-done.4.refs_2_ = bf16[512,512]{1,0:T(8,128)(2,1)S(1)} collective-permute-done((bf16[512,512]{1,0:T(8,128)(2,1)}, bf16[512,512]{1,0:T(8,128)(2,1)S(1)}, u32[]{:S(2)}, u32[]{:S(2)}) %collective-permute-start.4) | collective-permute-done | bytes 524320 | tf_op jit(solution)/shard_map/ppermute | solution.py:297
  67.3 3.8 %collective-permute-done.3.refs_1_ = bf16[512,512]{1,0:T(8,128)(2,1)S(1)} collective-permute-done((bf16[512,512]{1,0:T(8,128)(2,1)}, bf16[512,512]{1,0:T(8,128)(2,1)S(1)}, u32[]{:S(2)}, u32[]{:S(2)}) %collective-permute-start.3) | collective-permute-done | bytes 524320 | tf_op jit(solution)/shard_map/ppermute | solution.py:297
  71.1 0.0 collective-permute-start.5
  71.1 3.2 %collective-permute-start.6 = (bf16[512,512]{1,0:T(8,128)(2,1)}, bf16[512,512]{1,0:T(8,128)(2,1)S(1)}, u32[]{:S(2)}, u32[]{:S(2)}) collective-permute-start(bf16[512,512]{1,0:T(8,128)(2,1)} %get-tuple-element.34.refs_0_.refs_9_), channel_id=1, source_target_pairs={{0,3},{1,0},{2,1},{3,2},{4,7},{5,4},{6,5},{7,6},{8,11},{9,8},{10,9... | collective-permute-start | bytes 1572872 | tf_op jit(solution)/shard_map/ppermute | solution.py:297
  74.3 0.7 slice.47
  75.0 0.0 collective-permute-start.10
  75.0 0.7 slice.46
  75.7 2.0 %collective-permute-start.9 = (bf16[256,512]{1,0:T(8,128)(2,1)}, bf16[256,512]{1,0:T(8,128)(2,1)}, u32[]{:S(2)}, u32[]{:S(2)}) collective-permute-start(bf16[256,512]{1,0:T(8,128)(2,1)} %slice.46), channel_id=1, source_target_pairs={{0,1},{1,2},{2,3},{3,0},{4,5},{5,6},{6,7},{7,4},{8,9},{9,10},{10,1... | collective-permute-start | bytes 786440 | tf_op jit(solution)/shard_map/ppermute | solution.py:297
  77.8 9.5 %collective-permute-done.5.refs_1_ = bf16[512,512]{1,0:T(8,128)(2,1)S(1)} collective-permute-done((bf16[512,512]{1,0:T(8,128)(2,1)}, bf16[512,512]{1,0:T(8,128)(2,1)S(1)}, u32[]{:S(2)}, u32[]{:S(2)}) %collective-permute-start.5) | collective-permute-done | bytes 524320 | tf_op jit(solution)/shard_map/ppermute | solution.py:297
  87.3 0.8 slice.44
  88.1 0.0 collective-permute-start.7
  88.1 0.0 collective-permute-done.6.refs_2_
  88.1 0.8 slice.45
  88.8 3.2 %collective-permute-start.8 = (bf16[256,512]{1,0:T(8,128)(2,1)}, bf16[256,512]{1,0:T(8,128)(2,1)}, u32[]{:S(2)}, u32[]{:S(2)}) collective-permute-start(bf16[256,512]{1,0:T(8,128)(2,1)} %slice.45), channel_id=1, source_target_pairs={{0,3},{1,0},{2,1},{3,2},{4,7},{5,4},{6,5},{7,6},{8,11},{9,8},{10,9... | collective-permute-start | bytes 786440 | tf_op jit(solution)/shard_map/ppermute | solution.py:297
  92.2 0.2 copy.21.refs_13_.refs_10_
  92.4 0.6 collective-permute-done.9.refs_3_
  93.0 1.6 %copy-done = bf16[2048,512]{1,0:T(8,128)(2,1)S(1)} copy-done((bf16[2048,512]{1,0:T(8,128)(2,1)S(1)}, bf16[2048,512]{1,0:T(8,128)(2,1)}, u32[]{:S(2)}) %copy-start) | copy-done | bytes 2097176
  94.6 1.6 %copy-done.1 = bf16[2048,512]{1,0:T(8,128)(2,1)S(1)} copy-done((bf16[2048,512]{1,0:T(8,128)(2,1)S(1)}, bf16[2048,512]{1,0:T(8,128)(2,1)}, u32[]{:S(2)}) %copy-start.1) | copy-done | bytes 2097176
  96.2 1.0 copy-done.2
  97.2 1.0 copy-done.4
  98.3 1.0 copy-done.14
  99.3 1.0 copy-done.21
  100.3 1.0 copy-done.23
  101.4 6.8 %layer.2 = (bf16[512,512]{1,0:T(8,128)(2,1)S(1)}, bf16[512,512]{1,0:T(8,128)(2,1)S(1)}, bf16[512,512]{1,0:T(8,128)(2,1)S(1)}) custom-call(s32[1]{0:T(128)} %bitcast.group_ref, bf16[512,512]{1,0:T(8,128)(2,1)S(1)} %copy-done.14, bf16[512,512]{1,0:T(8,128)(2,1)S(1)} %copy-done.23, bf16[512,512]{1,0:T(8,128)(2,1)S(1)} %copy-done.21, ...), custom_call_target="tpu_custom_call" | custom-call | tf_op jit(solution)/shard_map/layer/pallas_call | solution.py:200
  108.2 0.1 collective-permute-start.15
  108.3 3.2 %collective-permute-start.16 = (bf16[512,512]{1,0:T(8,128)(2,1)S(1)}, bf16[512,512]{1,0:T(8,128)(2,1)S(1)}, u32[]{:S(2)}, u32[]{:S(2)}) collective-permute-start(bf16[512,512]{1,0:T(8,128)(2,1)S(1)} %get-tuple-element.48.refs_0_), channel_id=1, source_target_pairs={{0,3},{1,0},{2,1},{3,2},{4,7},{5,4},{6,5},{7,6},{8,11},{9,8},{10,9... | collective-permute-start | bytes 1572872 | tf_op jit(solution)/shard_map/ppermute | solution.py:297
  111.6 0.0 collective-permute-done.8.refs_4_
  111.6 0.0 copy-start.6
  111.6 8.0 %layer.3 = (bf16[512,512]{1,0:T(8,128)(2,1)S(1)}, bf16[512,512]{1,0:T(8,128)(2,1)S(1)}, bf16[512,512]{1,0:T(8,128)(2,1)S(1)}) custom-call(s32[1]{0:T(128)} %bitcast.group_ref, bf16[512,512]{1,0:T(8,128)(2,1)S(1)} %copy-done.13, bf16[512,512]{1,0:T(8,128)(2,1)S(1)} %copy-done.17, bf16[512,512]{1,0:T(8,128)(2,1)S(1)} %copy-done.19, ...), custom_call_target="tpu_custom_call" | custom-call | tf_op jit(solution)/shard_map/layer/pallas_call | solution.py:200
  119.6 0.0 copy-start.28
  119.6 0.1 collective-permute-start.11
  119.7 3.2 %collective-permute-start.12 = (bf16[512,512]{1,0:T(8,128)(2,1)S(1)}, bf16[512,512]{1,0:T(8,128)(2,1)S(1)}, u32[]{:S(2)}, u32[]{:S(2)}) collective-permute-start(bf16[512,512]{1,0:T(8,128)(2,1)S(1)} %get-tuple-element.43.refs_0_), channel_id=1, source_target_pairs={{0,3},{1,0},{2,1},{3,2},{4,7},{5,4},{6,5},{7,6},{8,11},{9,8},{10,9... | collective-permute-start | bytes 1572872 | tf_op jit(solution)/shard_map/ppermute | solution.py:297
  122.9 0.0 collective-permute-done.15.refs_1_
  123.0 0.1 collective-permute-start.17
  123.1 3.3 %collective-permute-start.18 = (bf16[256,512]{1,0:T(8,128)(2,1)S(1)}, bf16[256,512]{1,0:T(8,128)(2,1)S(1)}, u32[]{:S(2)}, u32[]{:S(2)}) collective-permute-start(bf16[256,512]{1,0:T(8,128)(2,1)S(1)} %slice.51), channel_id=1, source_target_pairs={{0,3},{1,0},{2,1},{3,2},{4,7},{5,4},{6,5},{7,6},{8,11},{9,8},{10,9... | collective-permute-start | bytes 786440 | tf_op jit(solution)/shard_map/ppermute | solution.py:297
  126.4 9.4 %collective-permute-done.11.refs_1_ = bf16[512,512]{1,0:T(8,128)(2,1)S(1)} collective-permute-done((bf16[512,512]{1,0:T(8,128)(2,1)S(1)}, bf16[512,512]{1,0:T(8,128)(2,1)S(1)}, u32[]{:S(2)}, u32[]{:S(2)}) %collective-permute-start.11) | collective-permute-done | bytes 524320 | tf_op jit(solution)/shard_map/ppermute | solution.py:297
  135.8 0.1 collective-permute-start.13
  135.9 0.0 collective-permute-done.12.refs_2_
  135.9 3.3 %collective-permute-start.14 = (bf16[256,512]{1,0:T(8,128)(2,1)S(1)}, bf16[256,512]{1,0:T(8,128)(2,1)S(1)}, u32[]{:S(2)}, u32[]{:S(2)}) collective-permute-start(bf16[256,512]{1,0:T(8,128)(2,1)S(1)} %slice.49), channel_id=1, source_target_pairs={{0,3},{1,0},{2,1},{3,2},{4,7},{5,4},{6,5},{7,6},{8,11},{9,8},{10,9... | collective-permute-start | bytes 786440 | tf_op jit(solution)/shard_map/ppermute | solution.py:297
  139.3 0.0 copy-start.15
  139.3 9.5 %pool.1 = bf16[16384,128]{1,0:T(8,128)(2,1)} custom-call(s32[1,1024]{1,0:T(1,128)S(1)} %bitcast.25, bf16[16384,128]{1,0:T(8,128)(2,1)S(1)} %bitcast.21, bf16[512,512]{1,0:T(8,128)(2,1)S(1)} %get-tuple-element.41.refs_14_.refs_0_, bf16[512,512]{1,0:T(8,128)(2,1)S(1)} %get-tuple-element.50.refs_1_, bf16[512,512]{1,0:T(8,128)(2,1)S(1)} %get-tuple-element.42.refs_15_.refs_2_, ...), custom_call_target="tpu_custom_call" | custom-call | tf_op jit(solution)/shard_map/pool/pallas_call | solution.py:282
  148.8 2.0 %finish.2.refs_11_ = bf16[1024,512]{1,0:T(8,128)(2,1)} custom-call(bf16[512,512]{1,0:T(8,128)(2,1)S(1)} %get-tuple-element.48.refs_0_, bf16[512,512]{1,0:T(8,128)(2,1)S(1)} %collective-permute-done.15.refs_1_, bf16[512,512]{1,0:T(8,128)(2,1)S(1)} %collective-permute-done.16.refs_2_, bf16[256,512]{1,0:T(8,128)(2,1)S(1)} %collective-permute-done.17.refs_3_, ...), custom_call_target="tpu_custom_call" | custom-call | tf_op jit(solution)/shard_map/finish/pallas_call | solution.py:236
  150.9 0.0 collective-permute-done.13.refs_3_
  150.9 0.0 collective-permute-done.14.refs_4_
  150.9 2.1 %finish.3 = bf16[1024,512]{1,0:T(8,128)(2,1)} custom-call(bf16[512,512]{1,0:T(8,128)(2,1)S(1)} %get-tuple-element.43.refs_0_, bf16[512,512]{1,0:T(8,128)(2,1)S(1)} %collective-permute-done.11.refs_1_, bf16[512,512]{1,0:T(8,128)(2,1)S(1)} %collective-permute-done.12.refs_2_, ...), custom_call_target="tpu_custom_call", output_to_operand_aliasing={{}: (11, {})} | custom-call | tf_op jit(solution)/shard_map/finish/pallas_call | solution.py:236
  (60 shorter events, 0.2 us)
Async XLA Ops:
  0.6 16.7 %copy-start.25 = (bf16[512,2048]{1,0:T(8,128)(2,1)S(1)}, bf16[512,2048]{1,0:T(8,128)(2,1)}, u32[]{:S(2)}) copy-start(bf16[512,2048]{1,0:T(8,128)(2,1)} %param.16) | copy-start | bytes 6291460
  5.1 42.1 %all-to-all-start = ((bf16[64,72,128]{2,1,0:T(8,128)(2,1)}), bf16[64,72,128]{2,1,0:T(8,128)(2,1)}, u32[]{:S(2)}, u32[]{:S(2)}) async-start(bf16[64,72,128]{2,1,0:T(8,128)(2,1)} %pack.1), calls=%async_computation | async-start | bytes 2359296 | tf_op jit(solution)/shard_map/all_to_all | solution.py:342
  17.3 6.2 %copy-start.24 = (s32[1024]{0:T(1024)S(1)}, s32[1024]{0:T(1024)}, u32[]{:S(2)}) copy-start(s32[1024]{0:T(1024)} %param.11) | copy-start | bytes 12292
  17.6 15.3 %collective-permute-start = (bf16[512,512]{1,0:T(8,128)(2,1)S(1)}, bf16[512,512]{1,0:T(8,128)(2,1)S(1)}, u32[]{:S(2)}, u32[]{:S(2)}) collective-permute-start(bf16[512,512]{1,0:T(8,128)(2,1)S(1)} %get-tuple-element.57), channel_id=1, source_target_pairs={{0,1},{1,2},{2,3},{3,0},{4,5},{5,6},{6,7},{7,4},{8,9},{9,10},{10,1... | collective-permute-start | bytes 1572872 | tf_op jit(solution)/shard_map/ppermute | solution.py:297
  19.2 26.1 %collective-permute-start.1 = (bf16[512,512]{1,0:T(8,128)(2,1)S(1)}, bf16[512,512]{1,0:T(8,128)(2,1)S(1)}, u32[]{:S(2)}, u32[]{:S(2)}) collective-permute-start(bf16[512,512]{1,0:T(8,128)(2,1)S(1)} %get-tuple-element.56), channel_id=1, source_target_pairs={{0,2},{1,3},{2,0},{3,1},{4,6},{5,7},{6,4},{7,5},{8,10},{9,11},{10,... | collective-permute-start | bytes 1572872 | tf_op jit(solution)/shard_map/ppermute | solution.py:297
  22.1 24.0 %collective-permute-start.2 = (bf16[512,512]{1,0:T(8,128)(2,1)S(1)}, bf16[512,512]{1,0:T(8,128)(2,1)S(1)}, u32[]{:S(2)}, u32[]{:S(2)}) collective-permute-start(bf16[512,512]{1,0:T(8,128)(2,1)S(1)} %get-tuple-element.55), channel_id=1, source_target_pairs={{0,3},{1,0},{2,1},{3,2},{4,7},{5,4},{6,5},{7,6},{8,11},{9,8},{10,9... | collective-permute-start | bytes 1572872 | tf_op jit(solution)/shard_map/ppermute | solution.py:297
  32.5 59.6 %copy-start.26 = (bf16[2048]{0:T(1024)(128)(2,1)S(1)}, bf16[2048]{0:T(1024)(128)(2,1)}, u32[]{:S(2)}) copy-start(bf16[2048]{0:T(1024)(128)(2,1)} %param.13) | copy-start | bytes 12292
  32.5 59.7 %copy-start.27 = (bf16[2048]{0:T(1024)(128)(2,1)S(1)}, bf16[2048]{0:T(1024)(128)(2,1)}, u32[]{:S(2)}) copy-start(bf16[2048]{0:T(1024)(128)(2,1)} %param.14) | copy-start | bytes 12292
  32.9 59.2 %copy-start.7 = (bf16[512,512]{1,0:T(8,128)(2,1)}, bf16[512,512]{1,0:T(8,128)(2,1)S(1)}, u32[]{:S(2)}) copy-start(bf16[512,512]{1,0:T(8,128)(2,1)S(1)} %collective-permute-done.refs_6_) | copy-start | bytes 1572868
  45.3 0.8 copy-start.9
  46.1 0.8 copy-start.11
  51.9 15.4 %collective-permute-start.4 = (bf16[512,512]{1,0:T(8,128)(2,1)}, bf16[512,512]{1,0:T(8,128)(2,1)S(1)}, u32[]{:S(2)}, u32[]{:S(2)}) collective-permute-start(bf16[512,512]{1,0:T(8,128)(2,1)} %get-tuple-element.33.refs_0_.refs_9_), channel_id=1, source_target_pairs={{0,3},{1,0},{2,1},{3,2},{4,7},{5,4},{6,5},{7,6},{8,11},{9,8},{10,9... | collective-permute-start | bytes 1572872 | tf_op jit(solution)/shard_map/ppermute | solution.py:297
  54.9 16.1 %collective-permute-start.3 = (bf16[512,512]{1,0:T(8,128)(2,1)}, bf16[512,512]{1,0:T(8,128)(2,1)S(1)}, u32[]{:S(2)}, u32[]{:S(2)}) collective-permute-start(bf16[512,512]{1,0:T(8,128)(2,1)} %get-tuple-element.33.refs_0_.refs_9_), channel_id=1, source_target_pairs={{0,1},{1,2},{2,3},{3,0},{4,5},{5,6},{6,7},{7,4},{8,9},{9,10},{10,1... | collective-permute-start | bytes 1572872 | tf_op jit(solution)/shard_map/ppermute | solution.py:297
  67.3 24.8 %copy-start.20 = (bf16[512,512]{1,0:T(8,128)(2,1)}, bf16[512,512]{1,0:T(8,128)(2,1)S(1)}, u32[]{:S(2)}) copy-start(bf16[512,512]{1,0:T(8,128)(2,1)S(1)} %collective-permute-done.4.refs_2_) | copy-start | bytes 1572868
  71.1 21.0 %copy-start.22 = (bf16[512,512]{1,0:T(8,128)(2,1)}, bf16[512,512]{1,0:T(8,128)(2,1)S(1)}, u32[]{:S(2)}) copy-start(bf16[512,512]{1,0:T(8,128)(2,1)S(1)} %collective-permute-done.3.refs_1_) | copy-start | bytes 1572868
  71.1 16.2 %collective-permute-start.5 = (bf16[512,512]{1,0:T(8,128)(2,1)}, bf16[512,512]{1,0:T(8,128)(2,1)S(1)}, u32[]{:S(2)}, u32[]{:S(2)}) collective-permute-start(bf16[512,512]{1,0:T(8,128)(2,1)} %get-tuple-element.34.refs_0_.refs_9_), channel_id=1, source_target_pairs={{0,1},{1,2},{2,3},{3,0},{4,5},{5,6},{6,7},{7,4},{8,9},{9,10},{10,1... | collective-permute-start | bytes 1572872 | tf_op jit(solution)/shard_map/ppermute | solution.py:297
  71.1 17.0 %collective-permute-start.6 = (bf16[512,512]{1,0:T(8,128)(2,1)}, bf16[512,512]{1,0:T(8,128)(2,1)S(1)}, u32[]{:S(2)}, u32[]{:S(2)}) collective-permute-start(bf16[512,512]{1,0:T(8,128)(2,1)} %get-tuple-element.34.refs_0_.refs_9_), channel_id=1, source_target_pairs={{0,3},{1,0},{2,1},{3,2},{4,7},{5,4},{6,5},{7,6},{8,11},{9,8},{10,9... | collective-permute-start | bytes 1572872 | tf_op jit(solution)/shard_map/ppermute | solution.py:297
  75.0 17.4 %collective-permute-start.10 = (bf16[256,512]{1,0:T(8,128)(2,1)}, bf16[256,512]{1,0:T(8,128)(2,1)}, u32[]{:S(2)}, u32[]{:S(2)}) collective-permute-start(bf16[256,512]{1,0:T(8,128)(2,1)} %slice.47), channel_id=1, source_target_pairs={{0,3},{1,0},{2,1},{3,2},{4,7},{5,4},{6,5},{7,6},{8,11},{9,8},{10,9... | collective-permute-start | bytes 786440 | tf_op jit(solution)/shard_map/ppermute | solution.py:297
  75.7 17.3 %collective-permute-start.9 = (bf16[256,512]{1,0:T(8,128)(2,1)}, bf16[256,512]{1,0:T(8,128)(2,1)}, u32[]{:S(2)}, u32[]{:S(2)}) collective-permute-start(bf16[256,512]{1,0:T(8,128)(2,1)} %slice.46), channel_id=1, source_target_pairs={{0,1},{1,2},{2,3},{3,0},{4,5},{5,6},{6,7},{7,4},{8,9},{9,10},{10,1... | collective-permute-start | bytes 786440 | tf_op jit(solution)/shard_map/ppermute | solution.py:297
  87.3 4.9 %copy-start.16 = (bf16[512,512]{1,0:T(8,128)(2,1)}, bf16[512,512]{1,0:T(8,128)(2,1)S(1)}, u32[]{:S(2)}) copy-start(bf16[512,512]{1,0:T(8,128)(2,1)S(1)} %collective-permute-done.5.refs_1_) | copy-start | bytes 1572868
  88.1 23.5 %collective-permute-start.7 = (bf16[256,512]{1,0:T(8,128)(2,1)}, bf16[256,512]{1,0:T(8,128)(2,1)S(1)}, u32[]{:S(2)}, u32[]{:S(2)}) collective-permute-start(bf16[256,512]{1,0:T(8,128)(2,1)} %slice.44), channel_id=1, source_target_pairs={{0,1},{1,2},{2,3},{3,0},{4,5},{5,6},{6,7},{7,4},{8,9},{9,10},{10,1... | collective-permute-start | bytes 786440 | tf_op jit(solution)/shard_map/ppermute | solution.py:297
  88.1 4.1 %copy-start.18 = (bf16[512,512]{1,0:T(8,128)(2,1)}, bf16[512,512]{1,0:T(8,128)(2,1)S(1)}, u32[]{:S(2)}) copy-start(bf16[512,512]{1,0:T(8,128)(2,1)S(1)} %collective-permute-done.6.refs_2_) | copy-start | bytes 1572868
  88.8 22.7 %collective-permute-start.8 = (bf16[256,512]{1,0:T(8,128)(2,1)}, bf16[256,512]{1,0:T(8,128)(2,1)}, u32[]{:S(2)}, u32[]{:S(2)}) collective-permute-start(bf16[256,512]{1,0:T(8,128)(2,1)} %slice.45), channel_id=1, source_target_pairs={{0,3},{1,0},{2,1},{3,2},{4,7},{5,4},{6,5},{7,6},{8,11},{9,8},{10,9... | collective-permute-start | bytes 786440 | tf_op jit(solution)/shard_map/ppermute | solution.py:297
  93.0 1.6 %copy-start = (bf16[2048,512]{1,0:T(8,128)(2,1)S(1)}, bf16[2048,512]{1,0:T(8,128)(2,1)}, u32[]{:S(2)}) copy-start(bf16[2048,512]{1,0:T(8,128)(2,1)} %get-tuple-element.36.refs_6_) | copy-start | bytes 6291460
  94.6 1.6 %copy-start.1 = (bf16[2048,512]{1,0:T(8,128)(2,1)S(1)}, bf16[2048,512]{1,0:T(8,128)(2,1)}, u32[]{:S(2)}) copy-start(bf16[2048,512]{1,0:T(8,128)(2,1)} %get-tuple-element.35.refs_5_) | copy-start | bytes 6291460
  96.2 1.0 copy-start.2
  97.2 1.0 copy-start.4
  98.3 1.0 copy-start.14
  99.3 1.0 copy-start.21
  100.3 1.0 copy-start.23
  101.4 10.2 %copy-start.3 = (f32[1024,128]{1,0:T(8,128)S(1)}, f32[1024,128]{1,0:T(8,128)}, u32[]{:S(2)}) copy-start(f32[1024,128]{1,0:T(8,128)} %get-tuple-element.39.refs_11_) | copy-start | bytes 1572868
  101.4 10.2 %copy-start.5 = (f32[1024,128]{1,0:T(8,128)S(1)}, f32[1024,128]{1,0:T(8,128)}, u32[]{:S(2)}) copy-start(f32[1024,128]{1,0:T(8,128)} %get-tuple-element.38.refs_10_) | copy-start | bytes 1572868
  101.4 10.2 %copy-start.13 = (bf16[512,512]{1,0:T(8,128)(2,1)S(1)}, bf16[512,512]{1,0:T(8,128)(2,1)}, u32[]{:S(2)}) copy-start(bf16[512,512]{1,0:T(8,128)(2,1)} %get-tuple-element.34.refs_0_.refs_9_) | copy-start | bytes 1572868
  101.4 10.2 %copy-start.17 = (bf16[512,512]{1,0:T(8,128)(2,1)S(1)}, bf16[512,512]{1,0:T(8,128)(2,1)}, u32[]{:S(2)}) copy-start(bf16[512,512]{1,0:T(8,128)(2,1)} %copy-done.16) | copy-start | bytes 1572868
  101.4 10.2 %copy-start.19 = (bf16[512,512]{1,0:T(8,128)(2,1)S(1)}, bf16[512,512]{1,0:T(8,128)(2,1)}, u32[]{:S(2)}) copy-start(bf16[512,512]{1,0:T(8,128)(2,1)} %copy-done.18) | copy-start | bytes 1572868
  108.2 14.7 %collective-permute-start.15 = (bf16[512,512]{1,0:T(8,128)(2,1)S(1)}, bf16[512,512]{1,0:T(8,128)(2,1)S(1)}, u32[]{:S(2)}, u32[]{:S(2)}) collective-permute-start(bf16[512,512]{1,0:T(8,128)(2,1)S(1)} %get-tuple-element.48.refs_0_), channel_id=1, source_target_pairs={{0,1},{1,2},{2,3},{3,0},{4,5},{5,6},{6,7},{7,4},{8,9},{9,10},{10,1... | collective-permute-start | bytes 1572872 | tf_op jit(solution)/shard_map/ppermute | solution.py:297
  108.3 14.7 %collective-permute-start.16 = (bf16[512,512]{1,0:T(8,128)(2,1)S(1)}, bf16[512,512]{1,0:T(8,128)(2,1)S(1)}, u32[]{:S(2)}, u32[]{:S(2)}) collective-permute-start(bf16[512,512]{1,0:T(8,128)(2,1)S(1)} %get-tuple-element.48.refs_0_), channel_id=1, source_target_pairs={{0,3},{1,0},{2,1},{3,2},{4,7},{5,4},{6,5},{7,6},{8,11},{9,8},{10,9... | collective-permute-start | bytes 1572872 | tf_op jit(solution)/shard_map/ppermute | solution.py:297
  111.6 27.6 %copy-start.6 = (bf16[2048,2,512]{2,1,0:T(2,128)(2,1)S(1)}, bf16[2048,2,512]{2,1,0:T(2,128)(2,1)}, u32[]{:S(2)}) copy-start(bf16[2048,2,512]{2,1,0:T(2,128)(2,1)} %param.17) | copy-start | bytes 12582916
  119.6 19.6 %copy-start.28 = (s32[1024]{0:T(1024)S(1)}, s32[1024]{0:T(1024)}, u32[]{:S(2)}) copy-start(s32[1024]{0:T(1024)} %param.12) | copy-start | bytes 12292
  119.6 16.2 %collective-permute-start.11 = (bf16[512,512]{1,0:T(8,128)(2,1)S(1)}, bf16[512,512]{1,0:T(8,128)(2,1)S(1)}, u32[]{:S(2)}, u32[]{:S(2)}) collective-permute-start(bf16[512,512]{1,0:T(8,128)(2,1)S(1)} %get-tuple-element.43.refs_0_), channel_id=1, source_target_pairs={{0,1},{1,2},{2,3},{3,0},{4,5},{5,6},{6,7},{7,4},{8,9},{9,10},{10,1... | collective-permute-start | bytes 1572872 | tf_op jit(solution)/shard_map/ppermute | solution.py:297
  119.7 16.2 %collective-permute-start.12 = (bf16[512,512]{1,0:T(8,128)(2,1)S(1)}, bf16[512,512]{1,0:T(8,128)(2,1)S(1)}, u32[]{:S(2)}, u32[]{:S(2)}) collective-permute-start(bf16[512,512]{1,0:T(8,128)(2,1)S(1)} %get-tuple-element.43.refs_0_), channel_id=1, source_target_pairs={{0,3},{1,0},{2,1},{3,2},{4,7},{5,4},{6,5},{7,6},{8,11},{9,8},{10,9... | collective-permute-start | bytes 1572872 | tf_op jit(solution)/shard_map/ppermute | solution.py:297
  123.0 25.8 %collective-permute-start.17 = (bf16[256,512]{1,0:T(8,128)(2,1)S(1)}, bf16[256,512]{1,0:T(8,128)(2,1)S(1)}, u32[]{:S(2)}, u32[]{:S(2)}) collective-permute-start(bf16[256,512]{1,0:T(8,128)(2,1)S(1)} %slice.50), channel_id=1, source_target_pairs={{0,1},{1,2},{2,3},{3,0},{4,5},{5,6},{6,7},{7,4},{8,9},{9,10},{10,1... | collective-permute-start | bytes 786440 | tf_op jit(solution)/shard_map/ppermute | solution.py:297
  123.1 25.7 %collective-permute-start.18 = (bf16[256,512]{1,0:T(8,128)(2,1)S(1)}, bf16[256,512]{1,0:T(8,128)(2,1)S(1)}, u32[]{:S(2)}, u32[]{:S(2)}) collective-permute-start(bf16[256,512]{1,0:T(8,128)(2,1)S(1)} %slice.51), channel_id=1, source_target_pairs={{0,3},{1,0},{2,1},{3,2},{4,7},{5,4},{6,5},{7,6},{8,11},{9,8},{10,9... | collective-permute-start | bytes 786440 | tf_op jit(solution)/shard_map/ppermute | solution.py:297
  135.8 15.1 %collective-permute-start.13 = (bf16[256,512]{1,0:T(8,128)(2,1)S(1)}, bf16[256,512]{1,0:T(8,128)(2,1)S(1)}, u32[]{:S(2)}, u32[]{:S(2)}) collective-permute-start(bf16[256,512]{1,0:T(8,128)(2,1)S(1)} %slice.48), channel_id=1, source_target_pairs={{0,1},{1,2},{2,3},{3,0},{4,5},{5,6},{6,7},{7,4},{8,9},{9,10},{10,1... | collective-permute-start | bytes 786440 | tf_op jit(solution)/shard_map/ppermute | solution.py:297
  135.9 14.9 %collective-permute-start.14 = (bf16[256,512]{1,0:T(8,128)(2,1)S(1)}, bf16[256,512]{1,0:T(8,128)(2,1)S(1)}, u32[]{:S(2)}, u32[]{:S(2)}) collective-permute-start(bf16[256,512]{1,0:T(8,128)(2,1)S(1)} %slice.49), channel_id=1, source_target_pairs={{0,3},{1,0},{2,1},{3,2},{4,7},{5,4},{6,5},{7,6},{8,11},{9,8},{10,9... | collective-permute-start | bytes 786440 | tf_op jit(solution)/shard_map/ppermute | solution.py:297
  139.2 9.6 %copy-start.8 = (bf16[512,512]{1,0:T(8,128)(2,1)S(1)}, bf16[512,512]{1,0:T(8,128)(2,1)}, u32[]{:S(2)}) copy-start(bf16[512,512]{1,0:T(8,128)(2,1)} %copy-done.7) | copy-start | bytes 1572868
  139.2 9.5 %copy-start.10 = (bf16[512,512]{1,0:T(8,128)(2,1)S(1)}, bf16[512,512]{1,0:T(8,128)(2,1)}, u32[]{:S(2)}) copy-start(bf16[512,512]{1,0:T(8,128)(2,1)} %copy-done.9) | copy-start | bytes 1572868
  139.3 9.5 %copy-start.12 = (bf16[512,512]{1,0:T(8,128)(2,1)S(1)}, bf16[512,512]{1,0:T(8,128)(2,1)}, u32[]{:S(2)}) copy-start(bf16[512,512]{1,0:T(8,128)(2,1)} %copy-done.11) | copy-start | bytes 1572868
  139.3 9.5 %copy-start.15 = (bf16[512,512]{1,0:T(8,128)(2,1)S(1)}, bf16[512,512]{1,0:T(8,128)(2,1)}, u32[]{:S(2)}) copy-start(bf16[512,512]{1,0:T(8,128)(2,1)} %get-tuple-element.33.refs_0_.refs_9_) | copy-start | bytes 1572868
where the time goes:
time: 153 us
  waiting for transfers between devices  48.8 us (32%)
  starting transfers between devices  43 us (28%)
  Pallas kernels  37.6 us (25%)
  local copies, waits for them, and re-layouts  18.9 us (12%)
  other arithmetic  3.65 us (2%)
    ppermute x19, waiting for transfers between devices, shift(): lax.ppermute(values, 'tensor', [(i, (i + distance) % size) for i in range...  48.5 us
    ppermute x19, starting transfers between devices, shift(): lax.ppermute(values, 'tensor', [(i, (i + distance) % size) for i in range...  30.8 us
    pallas_call x2, Pallas kernels, layer(): pl.pallas_call(functools.partial(layer_kernel, number), grid_spec=pltpu.P...  14.8 us
    all_to_all x1, starting transfers between devices, shards(): got = lax.all_to_all(packed, 'req', split_axis=0, concat_axis=0, tiled=True)  12.2 us
    unnamed x58, local copies, waits for them, and re-layouts  10.1 us
    pallas_call x1, Pallas kernels, write_pool(): pl.pallas_call(pool_kernel, grid=(slots // step,), in_specs=[whole((1, ro...  9.5 us
    squeeze x1, local copies, waits for them, and re-layouts, shards(): weights = [projection[:, which, :] for which in range(3)]  5.29 us
    pallas_call x1, Pallas kernels, unpack(): pl.pallas_call(unpack_kernel, out_shape=[jax.ShapeDtypeStruct((chunk, wid...  4.69 us
  transfers between devices with their start and end apart: 20, of which 8 were waited for; matrix products, arithmetic and copies ran while one was open for 8% of the time, Pallas kernels for 17%

commit v1 on v0

--- a/solution.py
+++ b/solution.py
@@ -125,34 +125,45 @@
 
 
 def layer_kernel(number, group_ref, *refs):
-    own, left, right, far_top, far_bottom, *weights = refs[:8]
-    gain, bias, cosine, sine, segment_row, segment_col = refs[8:14]
-    rest = refs[14:]
-    past_keys, past_values, (context, keys_out, values_out) = (
-        rest[:number],
-        rest[number : 2 * number],
-        rest[2 * number :],
-    )
+    own, left, right, far_top, far_bottom, *weights_from = refs[:8]
+    cosine_from, sine_from, gain, bias, segment_row, segment_col = refs[8:14]
+    past_keys = refs[14 : 14 + number]
+    past_values = refs[14 + number : 14 + 2 * number]
+    context, keys_out, values_out, pieces_ref, weights_ref, cosine, sine, done = refs[14 + 2 * number :]
     chunk, width = own.shape
+    half = chunk // 2
     groups = gain.shape[1] // width
     me = group_ref[0]
-    pieces = [
-        own[...].astype(f32),
-        left[...].astype(f32),
-        jnp.concatenate([far_top[...], far_bottom[...]], axis=0).astype(f32),
-        right[...].astype(f32),
+    table_rows = pl.ds(number * chunk, chunk)
+    moves = [
+        (own, pieces_ref.at[0]),
+        (left, pieces_ref.at[1]),
+        (far_top, pieces_ref.at[2, pl.ds(0, half)]),
+        (far_bottom, pieces_ref.at[2, pl.ds(half, half)]),
+        (right, pieces_ref.at[3]),
+        *[(source, weights_ref.at[which]) for which, source in enumerate(weights_from)],
+        (cosine_from.at[table_rows], cosine),
+        (sine_from.at[table_rows], sine),
     ]
+    copies = [pltpu.make_async_copy(source, to, done.at[i]) for i, (source, to) in enumerate(moves)]
+    for copy in copies:
+        copy.start()
+    for copy in copies[:5]:
+        copy.wait()
+    pieces = [pieces_ref[i].astype(f32) for i in range(4)]
     total = sum(jnp.sum(piece, axis=1, keepdims=True) for piece in pieces)
     mean = total * (1.0 / (width * groups))
     centred = [piece - mean for piece in pieces]
     spread = sum(jnp.sum(piece * piece, axis=1, keepdims=True) for piece in centred)
     scale = lax.rsqrt(spread * (1.0 / (width * groups)) + norm_epsilon)
+    for copy in copies[5:]:
+        copy.wait()
     projected = [0.0, 0.0, 0.0]
     for offset, piece in enumerate(centred):
         source = lax.rem(me + groups - offset, groups)
         place = pl.ds(pl.multiple_of(source * width, width), width)
         normed = (piece * scale * gain[:, place].astype(f32) + bias[:, place].astype(f32)).astype(bf16)
-        projected = [total + dot(normed, weight[place, :]) for total, weight in zip(projected, weights)]
+        projected = [total + dot(normed, weights_ref[i, place, :]) for i, total in enumerate(projected)]
     raw_queries, raw_keys, raw_values = [total.astype(bf16) for total in projected]
     cos_part = cosine[...]
     sin_part = sine[...]
@@ -197,21 +208,30 @@
     chunk, width = pieces[0].shape
     by_chunk = lambda columns: pl.BlockSpec((chunk, columns), lambda i, g: (number, 0))
     rows = jax.ShapeDtypeStruct((chunk, width), bf16)
+    pieces, weights, cosine, sine = jax.tree.map(
+        lambda array: pltpu.with_memory_space_constraint(array, pltpu.MemorySpace.HBM), (pieces, weights, cosine, sine)
+    )
     return pl.pallas_call(
         functools.partial(layer_kernel, number),
         grid_spec=pltpu.PrefetchScalarGridSpec(
             num_scalar_prefetch=1,
             grid=(1,),
-            in_specs=[whole(piece.shape) for piece in pieces]
-            + [whole(array.shape) for array in (*weights, gain, bias)]
-            + [by_chunk(LANES), by_chunk(LANES), whole(segment_row.shape), by_chunk(1)]
+            in_specs=[pl.BlockSpec(memory_space=pltpu.MemorySpace.HBM)] * (len(pieces) + len(weights) + 2)
+            + [whole(gain.shape), whole(bias.shape), whole(segment_row.shape), by_chunk(1)]
             + [whole(rows.shape)] * (2 * number),
             out_specs=[whole(rows.shape)] * 3,
+            scratch_shapes=[
+                pltpu.VMEM((4, chunk, width), bf16),
+                pltpu.VMEM((len(weights), *weights[0].shape), bf16),
+                pltpu.VMEM((chunk, LANES), f32),
+                pltpu.VMEM((chunk, LANES), f32),
+                pltpu.SemaphoreType.DMA((len(pieces) + len(weights) + 2,)),
+            ],
         ),
         out_shape=[rows] * 3,
         compiler_params=pltpu.CompilerParams(vmem_limit_bytes=40 << 20),
         name="layer",
-    )(group, *pieces, *weights, gain, bias, cosine, sine, segment_row, segment_col, *keys, *values)
+    )(group, *pieces, *weights, cosine, sine, gain, bias, segment_row, segment_col, *keys, *values)
 
 
 def finish_kernel(*refs):
@@ -297,13 +317,6 @@
     return lax.ppermute(values, "tensor", [(i, (i + distance) % size) for i in range(size)])
 
 
-def gather_pieces(own):
-    half = own.shape[0] // 2
-    left = shift(own, 1)
-    right = shift(own, -1)
-    return own, left, right, shift(left[:half], 1), shift(right[half:], -1)
-
-
 def rotary_tables(segment_ids):
     row_count = segment_ids.shape[0]
     row_ids = jnp.arange(row_count, dtype=i32)
@@ -359,23 +372,34 @@
     )
 
     placed = unpack(got, row_count, width)
-    gathered = []
-    for chunk in placed:
-        if gathered:
-            chunk, _ = lax.optimization_barrier((chunk, gathered[-1][1:3]))
-        gathered.append(gather_pieces(chunk))
-    keys, values, contexts = [], [], []
-    for number in range(CHUNKS):
-        context, key, value = layer(
-            number, group, gathered[number], weights, gain, bias, cosine, sine, segment_row, segment_col, keys, values
-        )
-        keys.append(key)
-        values.append(value)
-        contexts.append(gather_pieces(context))
-    mixed = None
-    for number in range(CHUNKS):
-        mixed = finish(number, contexts[number], out_weights, placed[number], segment_col, mixed)
-    return (mixed, write_pool(live_slot, cache_pool, keys, values))
+    own, later = placed
+    half = own.shape[0] // 2
+    layer_args = (weights, gain, bias, cosine, sine, segment_row, segment_col)
+
+    def near(rows):
+        return shift(rows, 1), shift(rows, -1)
+
+    def far(left, right):
+        return shift(left, 1), shift(right, -1)
+
+    left0, right0 = near(own)
+    left0_half, right0_half, later = lax.optimization_barrier((left0[:half], right0[half:], later))
+    far0 = far(left0_half, right0_half)
+    left1, right1 = near(later)
+    context0, key0, value0 = layer(0, group, (own, left0, right0, *far0), *layer_args, [], [])
+    far1 = far(left1[:half], right1[half:])
+    *far1, context0 = lax.optimization_barrier((*far1, context0))
+    context_left0, context_right0 = near(context0)
+    context1, key1, value1 = layer(1, group, (later, left1, right1, *far1), *layer_args, [key0], [value0])
+    context_left0, context_right0, context1 = lax.optimization_barrier((context_left0, context_right0, context1))
+    context_far0 = far(context_left0[:half], context_right0[half:])
+    context_left1, context_right1 = near(context1)
+    new_pool = write_pool(live_slot, cache_pool, [key0, key1], [value0, value1])
+    context_left1, context_right1, new_pool = lax.optimization_barrier((context_left1, context_right1, new_pool))
+    context_far1 = far(context_left1[:half], context_right1[half:])
+    mixed = finish(0, (context0, context_left0, context_right0, *context_far0), out_weights, own, segment_col, None)
+    mixed = finish(1, (context1, context_left1, context_right1, *context_far1), out_weights, later, segment_col, mixed)
+    return (mixed, new_pool)
 
 
 def solution(mesh):

time: 153 us -> 143 us (0.935); the launches traced: 153 us -> 141 us
  waiting for transfers between devices: 48.8 us -> 41.1 us
  local copies, waits for them, and re-layouts: 18.9 us -> 12 us
  Pallas kernels: 37.6 us -> 40.4 us
    unnamed x58 -> x26, local copies, waits for them, and re-layouts: 10.1 us -> 1.26 us
    ppermute x19, waiting for transfers between devices: 48.5 us -> 40.6 us  [shift(): lax.ppermute(values, 'tensor', [(i, (i + distance) % size) for i in range...]
    pallas_call x2, Pallas kernels: 14.8 us -> 17.8 us  [layer(): pl.pallas_call(functools.partial(layer_kernel, number), grid_spec=pltpu.P...]
  transfers between devices with their start and end apart: 20 -> 20, of which waited for: 8 -> 8; matrix products, arithmetic and copies ran while one was open for 8% -> 10% of each run, Pallas kernels for 17% -> 21%
where the time goes in v1:
time: 143 us; the launch traced here: 141 us
  starting transfers between devices  43 us (30%)
  waiting for transfers between devices  41.1 us (29%)
  Pallas kernels  40.4 us (28%)
  local copies, waits for them, and re-layouts  12 us (8%)
  other arithmetic  3.67 us (3%)
    ppermute x19, waiting for transfers between devices, shift(): lax.ppermute(values, 'tensor', [(i, (i + distance) % size) for i in range...  40.6 us
    ppermute x19, starting transfers between devices, shift(): lax.ppermute(values, 'tensor', [(i, (i + distance) % size) for i in range...  30.9 us
    pallas_call x2, Pallas kernels, layer(): pl.pallas_call(functools.partial(layer_kernel, number), grid_spec=pltpu.P...  17.8 us
    all_to_all x1, starting transfers between devices, shards(): got = lax.all_to_all(packed, 'req', split_axis=0, concat_axis=0, tiled=True)  12 us
    pallas_call x1, Pallas kernels, write_pool(): pl.pallas_call(pool_kernel, grid=(slots // step,), in_specs=[whole((1, ro...  9.51 us
    squeeze x1, local copies, waits for them, and re-layouts, shards(): weights = [projection[:, which, :] for which in range(3)]  5.71 us
    pallas_call x1, Pallas kernels, unpack(): pl.pallas_call(unpack_kernel, out_shape=[jax.ShapeDtypeStruct((chunk, wid...  4.7 us
    pallas_call x1, Pallas kernels, pack(): pl.pallas_call(functools.partial(pack_kernel, peers=peers), out_shape=jax...  4.3 us
  transfers between devices with their start and end apart: 20, of which 8 were waited for; matrix products, arithmetic and copies ran while one was open for 10% of the time, Pallas kernels for 21%

profile of v1, /device:TPU:2, one launch (start us, length us, event | category | flops | bytes accessed | tf_op | source)
XLA Modules:
  0.0 141.0 jit_solution(15250337818080843313)
XLA Ops:
  0.6 4.3 %pack.1 = bf16[64,72,128]{2,1,0:T(8,128)(2,1)} custom-call(s32[1,1024]{1,0:T(1,128)} %bitcast.27, bf16[1024,512]{1,0:T(8,128)(2,1)} %stream_ref.1), custom_call_target="tpu_custom_call" | custom-call | tf_op jit(solution)/shard_map/pack/pallas_call | solution.py:90
  4.9 12.0 %all-to-all-start = ((bf16[64,72,128]{2,1,0:T(8,128)(2,1)}), bf16[64,72,128]{2,1,0:T(8,128)(2,1)S(1)}, u32[]{:S(2)}, u32[]{:S(2)}) async-start(bf16[64,72,128]{2,1,0:T(8,128)(2,1)} %pack.1), calls=%async_computation | async-start | bytes 2359296 | tf_op jit(solution)/shard_map/all_to_all | solution.py:355
  17.0 0.0 copy-start.3
  17.0 1.7 %constant_dynamic-slice_fusion = (bf16[512,512]{1,0:T(8,128)(2,1)S(1)}, bf16[512,512]{1,0:T(8,128)(2,1)S(1)}, bf16[512,512]{1,0:T(8,128)(2,1)S(1)}, bf16[512,512]{1,0:T(8,128)(2,1)S(1)}) fusion(bf16[512,2048]{1,0:T(8,128)(2,1)} %param.16, s32[]{:T(128)S(6)} %select_n.59, s32[]{:T(128)S(6)} %select_n.58, s32[]{:T(128)S(6)} %select_n.57, s32[]{:T(128)S(6)} %select_n.56), kind=kLoop, calls=%fused_computation.18 | loop fusion | bytes 4194320 | tf_op jit(solution)/shard_map/dynamic_slice | solution.py:367
  18.7 1.7 %collective-permute-start = (bf16[512,512]{1,0:T(8,128)(2,1)S(1)}, bf16[512,512]{1,0:T(8,128)(2,1)S(1)}, u32[]{:S(2)}, u32[]{:S(2)}) collective-permute-start(bf16[512,512]{1,0:T(8,128)(2,1)S(1)} %get-tuple-element.79), channel_id=1, source_target_pairs={{0,1},{1,2},{2,3},{3,0},{4,5},{5,6},{6,7},{7,4},{8,9},{9,10},{10,1... | collective-permute-start | bytes 1572872 | tf_op jit(solution)/shard_map/ppermute | solution.py:317
  20.4 2.9 %collective-permute-start.1 = (bf16[512,512]{1,0:T(8,128)(2,1)S(1)}, bf16[512,512]{1,0:T(8,128)(2,1)S(1)}, u32[]{:S(2)}, u32[]{:S(2)}) collective-permute-start(bf16[512,512]{1,0:T(8,128)(2,1)S(1)} %get-tuple-element.78), channel_id=1, source_target_pairs={{0,2},{1,3},{2,0},{3,1},{4,6},{5,7},{6,4},{7,5},{8,10},{9,11},{10,... | collective-permute-start | bytes 1572872 | tf_op jit(solution)/shard_map/ppermute | solution.py:317
  23.3 1.3 collective-permute-start.2
  24.6 0.0 copy-done.3
  24.6 0.5 convert_reduce_fusion
  25.2 3.1 %fusion.3 = (f32[1024,128]{1,0:T(8,128)}, f32[1024,128]{1,0:T(8,128)}) fusion(f32[128]{0:T(128)S(1)} %get-tuple-element.83, f32[128]{0:T(128)S(1)} %get-tuple-element.84, f32[1024]{0:T(1024)S(1)} %convert_element_type.18, pred[128]{0:T(512)(128)(4,1)S(1)} %iota_compare_fusion.1), kind=kLoop, calls=%fused_computation.10 | loop fusion | flops 524288 | bytes 1053824 | tf_op jit(solution)/shard_map/jit(_where)/select_n | solution.py:331
  28.3 5.7 %slice_bitcast_fusion = (bf16[2048,512]{1,0:T(8,128)(2,1)}, bf16[2048,512]{1,0:T(8,128)(2,1)}, bf16[2048,512]{1,0:T(8,128)(2,1)}) fusion(bf16[2048,3,512]{2,0,1:T(8,128)(2,1)} %param.15), kind=kLoop, calls=%fused_computation.3 | loop fusion | bytes 12582912 | tf_op jit(solution)/shard_map/squeeze | solution.py:357
  34.0 0.0 collective-permute-done.refs_6_
  34.0 12.4 %collective-permute-done.1.refs_7_ = bf16[512,512]{1,0:T(8,128)(2,1)S(1)} collective-permute-done((bf16[512,512]{1,0:T(8,128)(2,1)S(1)}, bf16[512,512]{1,0:T(8,128)(2,1)S(1)}, u32[]{:S(2)}, u32[]{:S(2)}) %collective-permute-start.1) | collective-permute-done | bytes 524320 | tf_op jit(solution)/shard_map/ppermute | solution.py:317
  46.4 0.0 collective-permute-done.2.refs_8_
  46.5 0.5 all-to-all-done.got_ref
  47.0 1.0 copy-done.4
  48.0 4.7 %unpack.1 = (bf16[512,512]{1,0:T(8,128)(2,1)}, bf16[512,512]{1,0:T(8,128)(2,1)}) custom-call(bf16[64,72,128]{2,1,0:T(8,128)(2,1)} %copy-done.4), custom_call_target="tpu_custom_call" | custom-call | tf_op jit(solution)/shard_map/unpack/pallas_call | solution.py:120
  52.7 1.6 %collective-permute-start.3 = (bf16[512,512]{1,0:T(8,128)(2,1)}, bf16[512,512]{1,0:T(8,128)(2,1)S(1)}, u32[]{:S(2)}, u32[]{:S(2)}) collective-permute-start(bf16[512,512]{1,0:T(8,128)(2,1)} %get-tuple-element.43.refs_0_.refs_9_), channel_id=1, source_target_pairs={{0,1},{1,2},{2,3},{3,0},{4,5},{5,6},{6,7},{7,4},{8,9},{9,10},{10,1... | collective-permute-start | bytes 1572872 | tf_op jit(solution)/shard_map/ppermute | solution.py:317
  54.3 1.7 %collective-permute-start.4 = (bf16[512,512]{1,0:T(8,128)(2,1)}, bf16[512,512]{1,0:T(8,128)(2,1)S(1)}, u32[]{:S(2)}, u32[]{:S(2)}) collective-permute-start(bf16[512,512]{1,0:T(8,128)(2,1)} %get-tuple-element.43.refs_0_.refs_9_), channel_id=1, source_target_pairs={{0,3},{1,0},{2,1},{3,2},{4,7},{5,4},{6,5},{7,6},{8,11},{9,8},{10,9... | collective-permute-start | bytes 1572872 | tf_op jit(solution)/shard_map/ppermute | solution.py:317
  56.0 12.6 %collective-permute-done.3.refs_1_ = bf16[512,512]{1,0:T(8,128)(2,1)S(1)} collective-permute-done((bf16[512,512]{1,0:T(8,128)(2,1)}, bf16[512,512]{1,0:T(8,128)(2,1)S(1)}, u32[]{:S(2)}, u32[]{:S(2)}) %collective-permute-start.3) | collective-permute-done | bytes 524320 | tf_op jit(solution)/shard_map/ppermute | solution.py:317
  68.6 0.8 slice.44
  69.4 0.0 collective-permute-done.4.refs_2_
  69.4 0.8 slice.45
  70.1 0.2 copy-done.8
  70.3 1.4 %collective-permute-start.5 = (bf16[512,512]{1,0:T(8,128)(2,1)}, bf16[512,512]{1,0:T(8,128)(2,1)S(1)}, u32[]{:S(2)}, u32[]{:S(2)}) collective-permute-start(bf16[512,512]{1,0:T(8,128)(2,1)} %get-tuple-element.45.refs_0_.refs_9_), channel_id=1, source_target_pairs={{0,1},{1,2},{2,3},{3,0},{4,5},{5,6},{6,7},{7,4},{8,9},{9,10},{10,1... | collective-permute-start | bytes 1572872 | tf_op jit(solution)/shard_map/ppermute | solution.py:317
  71.7 1.8 %collective-permute-start.7 = (bf16[512,512]{1,0:T(8,128)(2,1)}, bf16[512,512]{1,0:T(8,128)(2,1)S(1)}, u32[]{:S(2)}, u32[]{:S(2)}) collective-permute-start(bf16[512,512]{1,0:T(8,128)(2,1)} %get-tuple-element.45.refs_0_.refs_9_), channel_id=1, source_target_pairs={{0,3},{1,0},{2,1},{3,2},{4,7},{5,4},{6,5},{7,6},{8,11},{9,8},{10,9... | collective-permute-start | bytes 1572872 | tf_op jit(solution)/shard_map/ppermute | solution.py:317
  73.5 1.5 %collective-permute-start.10 = (bf16[256,512]{1,0:T(8,128)(2,1)}, bf16[256,512]{1,0:T(8,128)(2,1)}, u32[]{:S(2)}, u32[]{:S(2)}) collective-permute-start(bf16[256,512]{1,0:T(8,128)(2,1)} %slice.45), channel_id=1, source_target_pairs={{0,3},{1,0},{2,1},{3,2},{4,7},{5,4},{6,5},{7,6},{8,11},{9,8},{10,9... | collective-permute-start | bytes 786440 | tf_op jit(solution)/shard_map/ppermute | solution.py:317
  75.0 0.6 collective-permute-start.9
  75.6 10.9 %collective-permute-done.5.refs_1_ = bf16[512,512]{1,0:T(8,128)(2,1)S(1)} collective-permute-done((bf16[512,512]{1,0:T(8,128)(2,1)}, bf16[512,512]{1,0:T(8,128)(2,1)S(1)}, u32[]{:S(2)}, u32[]{:S(2)}) %collective-permute-start.5) | collective-permute-done | bytes 524320 | tf_op jit(solution)/shard_map/ppermute | solution.py:317
  86.5 0.8 slice.46
  87.3 0.2 collective-permute-start.6
  87.5 0.0 collective-permute-done.7.refs_2_
  87.5 0.8 slice.47
  88.2 3.0 %collective-permute-start.8 = (bf16[256,512]{1,0:T(8,128)(2,1)}, bf16[256,512]{1,0:T(8,128)(2,1)}, u32[]{:S(2)}, u32[]{:S(2)}) collective-permute-start(bf16[256,512]{1,0:T(8,128)(2,1)} %slice.47), channel_id=1, source_target_pairs={{0,3},{1,0},{2,1},{3,2},{4,7},{5,4},{6,5},{7,6},{8,11},{9,8},{10,9... | collective-permute-start | bytes 786440 | tf_op jit(solution)/shard_map/ppermute | solution.py:317
  91.3 0.0 copy-done.10
  91.3 0.2 copy.20.refs_13_.refs_10_
  91.5 1.0 collective-permute-done.10.refs_4_
  92.5 0.0 collective-permute-done.9.refs_3_
  92.5 0.0 copy-done.6
  92.5 8.3 %layer.2 = (bf16[512,512]{1,0:T(8,128)(2,1)S(1)}, bf16[512,512]{1,0:T(8,128)(2,1)S(1)}, bf16[512,512]{1,0:T(8,128)(2,1)S(1)}) custom-call(s32[1]{0:T(128)} %bitcast.5.group_ref, bf16[512,512]{1,0:T(8,128)(2,1)} %get-tuple-element.43.refs_0_.refs_9_, bf16[512,512]{1,0:T(8,128)(2,1)} %copy-done.7, bf16[512,512]{1,0:T(8,128)(2,1)} %copy-done.8, ...), custom_call_target="tpu_custom_call" | custom-call | tf_op jit(solution)/shard_map/layer/pallas_call | solution.py:214
  100.8 0.0 collective-permute-done.6.refs_3_
  100.8 0.0 collective-permute-done.8.refs_4_
  100.8 1.4 collective-permute-start.11
  102.1 2.0 %collective-permute-start.12 = (bf16[512,512]{1,0:T(8,128)(2,1)S(1)}, bf16[512,512]{1,0:T(8,128)(2,1)S(1)}, u32[]{:S(2)}, u32[]{:S(2)}) collective-permute-start(bf16[512,512]{1,0:T(8,128)(2,1)S(1)} %get-tuple-element.55.refs_0_), channel_id=1, source_target_pairs={{0,3},{1,0},{2,1},{3,2},{4,7},{5,4},{6,5},{7,6},{8,11},{9,8},{10,9... | collective-permute-start | bytes 1572872 | tf_op jit(solution)/shard_map/ppermute | solution.py:317
  104.1 0.0 copy-done.9
  104.1 9.6 %layer.3 = (bf16[512,512]{1,0:T(8,128)(2,1)S(1)}, bf16[512,512]{1,0:T(8,128)(2,1)S(1)}, bf16[512,512]{1,0:T(8,128)(2,1)S(1)}) custom-call(s32[1]{0:T(128)} %bitcast.5.group_ref, bf16[512,512]{1,0:T(8,128)(2,1)} %get-tuple-element.45.refs_0_.refs_9_, bf16[512,512]{1,0:T(8,128)(2,1)} %copy-done.5, bf16[512,512]{1,0:T(8,128)(2,1)} %copy-done.6, ...), custom_call_target="tpu_custom_call" | custom-call | tf_op jit(solution)/shard_map/layer/pallas_call | solution.py:214
  113.7 0.5 collective-permute-done.11.refs_1_
  114.2 0.0 collective-permute-done.12.refs_2_
  114.2 0.8 collective-permute-start.13
  115.0 2.4 %collective-permute-start.14 = (bf16[512,512]{1,0:T(8,128)(2,1)S(1)}, bf16[512,512]{1,0:T(8,128)(2,1)S(1)}, u32[]{:S(2)}, u32[]{:S(2)}) collective-permute-start(bf16[512,512]{1,0:T(8,128)(2,1)S(1)} %get-tuple-element.61.refs_0_), channel_id=1, source_target_pairs={{0,3},{1,0},{2,1},{3,2},{4,7},{5,4},{6,5},{7,6},{8,11},{9,8},{10,9... | collective-permute-start | bytes 1572872 | tf_op jit(solution)/shard_map/ppermute | solution.py:317
  117.4 0.0 copy-done.12
  117.4 9.5 %pool.1 = bf16[16384,128]{1,0:T(8,128)(2,1)} custom-call(s32[1,1024]{1,0:T(1,128)S(1)} %bitcast.25, bf16[16384,128]{1,0:T(8,128)(2,1)S(1)} %bitcast.21, bf16[512,512]{1,0:T(8,128)(2,1)S(1)} %get-tuple-element.58.refs_14_.refs_0_, bf16[512,512]{1,0:T(8,128)(2,1)S(1)} %get-tuple-element.63.refs_1_, bf16[512,512]{1,0:T(8,128)(2,1)S(1)} %get-tuple-element.59.refs_15_.refs_2_, ...), custom_call_target="tpu_custom_call" | custom-call | tf_op jit(solution)/shard_map/pool/pallas_call | solution.py:302
  127.0 0.1 collective-permute-start.17
  127.1 3.3 %collective-permute-start.18 = (bf16[256,512]{1,0:T(8,128)(2,1)S(1)}, bf16[256,512]{1,0:T(8,128)(2,1)S(1)}, u32[]{:S(2)}, u32[]{:S(2)}) collective-permute-start(bf16[256,512]{1,0:T(8,128)(2,1)S(1)} %slice.43), channel_id=1, source_target_pairs={{0,3},{1,0},{2,1},{3,2},{4,7},{5,4},{6,5},{7,6},{8,11},{9,8},{10,9... | collective-permute-start | bytes 786440 | tf_op jit(solution)/shard_map/ppermute | solution.py:317
  130.4 0.0 collective-permute-done.13.refs_1_
  130.4 0.0 collective-permute-done.14.refs_2_
  130.4 0.1 collective-permute-start.15
  130.5 3.3 %collective-permute-start.16 = (bf16[256,512]{1,0:T(8,128)(2,1)S(1)}, bf16[256,512]{1,0:T(8,128)(2,1)S(1)}, u32[]{:S(2)}, u32[]{:S(2)}) collective-permute-start(bf16[256,512]{1,0:T(8,128)(2,1)S(1)} %slice.41), channel_id=1, source_target_pairs={{0,3},{1,0},{2,1},{3,2},{4,7},{5,4},{6,5},{7,6},{8,11},{9,8},{10,9... | collective-permute-start | bytes 786440 | tf_op jit(solution)/shard_map/ppermute | solution.py:317
  133.8 2.3 %collective-permute-done.17.refs_3_ = bf16[256,512]{1,0:T(8,128)(2,1)S(1)} collective-permute-done((bf16[256,512]{1,0:T(8,128)(2,1)S(1)}, bf16[256,512]{1,0:T(8,128)(2,1)S(1)}, u32[]{:S(2)}, u32[]{:S(2)}) %collective-permute-start.17) | collective-permute-done | bytes 262176 | tf_op jit(solution)/shard_map/ppermute | solution.py:317
  136.2 0.0 collective-permute-done.18.refs_4_
  136.2 2.0 %finish.2.refs_11_ = bf16[1024,512]{1,0:T(8,128)(2,1)} custom-call(bf16[512,512]{1,0:T(8,128)(2,1)S(1)} %get-tuple-element.55.refs_0_, bf16[512,512]{1,0:T(8,128)(2,1)S(1)} %collective-permute-done.11.refs_1_, bf16[512,512]{1,0:T(8,128)(2,1)S(1)} %collective-permute-done.12.refs_2_, bf16[256,512]{1,0:T(8,128)(2,1)S(1)} %collective-permute-done.17.refs_3_, ...), custom_call_target="tpu_custom_call" | custom-call | tf_op jit(solution)/shard_map/finish/pallas_call | solution.py:256
  138.2 0.8 collective-permute-done.15.refs_3_
  139.0 0.0 collective-permute-done.16.refs_4_
  139.0 2.0 %finish.3 = bf16[1024,512]{1,0:T(8,128)(2,1)} custom-call(bf16[512,512]{1,0:T(8,128)(2,1)S(1)} %get-tuple-element.61.refs_0_, bf16[512,512]{1,0:T(8,128)(2,1)S(1)} %collective-permute-done.13.refs_1_, bf16[512,512]{1,0:T(8,128)(2,1)S(1)} %collective-permute-done.14.refs_2_, ...), custom_call_target="tpu_custom_call", output_to_operand_aliasing={{}: (11, {})} | custom-call | tf_op jit(solution)/shard_map/finish/pallas_call | solution.py:256
  (28 shorter events, 0.1 us)
Async XLA Ops:
  4.9 42.0 %all-to-all-start = ((bf16[64,72,128]{2,1,0:T(8,128)(2,1)}), bf16[64,72,128]{2,1,0:T(8,128)(2,1)S(1)}, u32[]{:S(2)}, u32[]{:S(2)}) async-start(bf16[64,72,128]{2,1,0:T(8,128)(2,1)} %pack.1), calls=%async_computation | async-start | bytes 2359296 | tf_op jit(solution)/shard_map/all_to_all | solution.py:355
  17.0 7.6 %copy-start.3 = (s32[1024]{0:T(1024)S(1)}, s32[1024]{0:T(1024)}, u32[]{:S(2)}) copy-start(s32[1024]{0:T(1024)} %param.11) | copy-start | bytes 12292
  18.7 15.3 %collective-permute-start = (bf16[512,512]{1,0:T(8,128)(2,1)S(1)}, bf16[512,512]{1,0:T(8,128)(2,1)S(1)}, u32[]{:S(2)}, u32[]{:S(2)}) collective-permute-start(bf16[512,512]{1,0:T(8,128)(2,1)S(1)} %get-tuple-element.79), channel_id=1, source_target_pairs={{0,1},{1,2},{2,3},{3,0},{4,5},{5,6},{6,7},{7,4},{8,9},{9,10},{10,1... | collective-permute-start | bytes 1572872 | tf_op jit(solution)/shard_map/ppermute | solution.py:317
  20.4 26.1 %collective-permute-start.1 = (bf16[512,512]{1,0:T(8,128)(2,1)S(1)}, bf16[512,512]{1,0:T(8,128)(2,1)S(1)}, u32[]{:S(2)}, u32[]{:S(2)}) collective-permute-start(bf16[512,512]{1,0:T(8,128)(2,1)S(1)} %get-tuple-element.78), channel_id=1, source_target_pairs={{0,2},{1,3},{2,0},{3,1},{4,6},{5,7},{6,4},{7,5},{8,10},{9,11},{10,... | collective-permute-start | bytes 1572872 | tf_op jit(solution)/shard_map/ppermute | solution.py:317
  23.3 23.2 %collective-permute-start.2 = (bf16[512,512]{1,0:T(8,128)(2,1)S(1)}, bf16[512,512]{1,0:T(8,128)(2,1)S(1)}, u32[]{:S(2)}, u32[]{:S(2)}) collective-permute-start(bf16[512,512]{1,0:T(8,128)(2,1)S(1)} %get-tuple-element.77), channel_id=1, source_target_pairs={{0,3},{1,0},{2,1},{3,2},{4,7},{5,4},{6,5},{7,6},{8,11},{9,8},{10,9... | collective-permute-start | bytes 1572872 | tf_op jit(solution)/shard_map/ppermute | solution.py:317
  34.0 57.2 %copy-start.10 = (bf16[2048]{0:T(1024)(128)(2,1)S(1)}, bf16[2048]{0:T(1024)(128)(2,1)}, u32[]{:S(2)}) copy-start(bf16[2048]{0:T(1024)(128)(2,1)} %param.13) | copy-start | bytes 12292
  34.0 57.3 %copy-start.11 = (bf16[2048]{0:T(1024)(128)(2,1)S(1)}, bf16[2048]{0:T(1024)(128)(2,1)}, u32[]{:S(2)}) copy-start(bf16[2048]{0:T(1024)(128)(2,1)} %param.14) | copy-start | bytes 12292
  47.0 1.1 copy-start.4
  52.7 15.9 %collective-permute-start.3 = (bf16[512,512]{1,0:T(8,128)(2,1)}, bf16[512,512]{1,0:T(8,128)(2,1)S(1)}, u32[]{:S(2)}, u32[]{:S(2)}) collective-permute-start(bf16[512,512]{1,0:T(8,128)(2,1)} %get-tuple-element.43.refs_0_.refs_9_), channel_id=1, source_target_pairs={{0,1},{1,2},{2,3},{3,0},{4,5},{5,6},{6,7},{7,4},{8,9},{9,10},{10,1... | collective-permute-start | bytes 1572872 | tf_op jit(solution)/shard_map/ppermute | solution.py:317
  54.3 15.1 %collective-permute-start.4 = (bf16[512,512]{1,0:T(8,128)(2,1)}, bf16[512,512]{1,0:T(8,128)(2,1)S(1)}, u32[]{:S(2)}, u32[]{:S(2)}) collective-permute-start(bf16[512,512]{1,0:T(8,128)(2,1)} %get-tuple-element.43.refs_0_.refs_9_), channel_id=1, source_target_pairs={{0,3},{1,0},{2,1},{3,2},{4,7},{5,4},{6,5},{7,6},{8,11},{9,8},{10,9... | collective-permute-start | bytes 1572872 | tf_op jit(solution)/shard_map/ppermute | solution.py:317
  68.6 1.5 %copy-start.7 = (bf16[512,512]{1,0:T(8,128)(2,1)}, bf16[512,512]{1,0:T(8,128)(2,1)S(1)}, u32[]{:S(2)}) copy-start(bf16[512,512]{1,0:T(8,128)(2,1)S(1)} %collective-permute-done.3.refs_1_) | copy-start | bytes 1572868
  69.4 0.9 copy-start.8
  70.3 16.2 %collective-permute-start.5 = (bf16[512,512]{1,0:T(8,128)(2,1)}, bf16[512,512]{1,0:T(8,128)(2,1)S(1)}, u32[]{:S(2)}, u32[]{:S(2)}) collective-permute-start(bf16[512,512]{1,0:T(8,128)(2,1)} %get-tuple-element.45.refs_0_.refs_9_), channel_id=1, source_target_pairs={{0,1},{1,2},{2,3},{3,0},{4,5},{5,6},{6,7},{7,4},{8,9},{9,10},{10,1... | collective-permute-start | bytes 1572872 | tf_op jit(solution)/shard_map/ppermute | solution.py:317
  71.7 15.7 %collective-permute-start.7 = (bf16[512,512]{1,0:T(8,128)(2,1)}, bf16[512,512]{1,0:T(8,128)(2,1)S(1)}, u32[]{:S(2)}, u32[]{:S(2)}) collective-permute-start(bf16[512,512]{1,0:T(8,128)(2,1)} %get-tuple-element.45.refs_0_.refs_9_), channel_id=1, source_target_pairs={{0,3},{1,0},{2,1},{3,2},{4,7},{5,4},{6,5},{7,6},{8,11},{9,8},{10,9... | collective-permute-start | bytes 1572872 | tf_op jit(solution)/shard_map/ppermute | solution.py:317
  73.5 18.9 %collective-permute-start.10 = (bf16[256,512]{1,0:T(8,128)(2,1)}, bf16[256,512]{1,0:T(8,128)(2,1)}, u32[]{:S(2)}, u32[]{:S(2)}) collective-permute-start(bf16[256,512]{1,0:T(8,128)(2,1)} %slice.45), channel_id=1, source_target_pairs={{0,3},{1,0},{2,1},{3,2},{4,7},{5,4},{6,5},{7,6},{8,11},{9,8},{10,9... | collective-permute-start | bytes 786440 | tf_op jit(solution)/shard_map/ppermute | solution.py:317
  75.0 17.5 %collective-permute-start.9 = (bf16[256,512]{1,0:T(8,128)(2,1)}, bf16[256,512]{1,0:T(8,128)(2,1)}, u32[]{:S(2)}, u32[]{:S(2)}) collective-permute-start(bf16[256,512]{1,0:T(8,128)(2,1)} %slice.44), channel_id=1, source_target_pairs={{0,1},{1,2},{2,3},{3,0},{4,5},{5,6},{6,7},{7,4},{8,9},{9,10},{10,1... | collective-permute-start | bytes 786440 | tf_op jit(solution)/shard_map/ppermute | solution.py:317
  86.5 4.8 %copy-start.5 = (bf16[512,512]{1,0:T(8,128)(2,1)}, bf16[512,512]{1,0:T(8,128)(2,1)S(1)}, u32[]{:S(2)}) copy-start(bf16[512,512]{1,0:T(8,128)(2,1)S(1)} %collective-permute-done.5.refs_1_) | copy-start | bytes 1572868
  87.3 13.5 %collective-permute-start.6 = (bf16[256,512]{1,0:T(8,128)(2,1)}, bf16[256,512]{1,0:T(8,128)(2,1)S(1)}, u32[]{:S(2)}, u32[]{:S(2)}) collective-permute-start(bf16[256,512]{1,0:T(8,128)(2,1)} %slice.46), channel_id=1, source_target_pairs={{0,1},{1,2},{2,3},{3,0},{4,5},{5,6},{6,7},{7,4},{8,9},{9,10},{10,1... | collective-permute-start | bytes 786440 | tf_op jit(solution)/shard_map/ppermute | solution.py:317
  87.5 5.0 %copy-start.6 = (bf16[512,512]{1,0:T(8,128)(2,1)}, bf16[512,512]{1,0:T(8,128)(2,1)S(1)}, u32[]{:S(2)}) copy-start(bf16[512,512]{1,0:T(8,128)(2,1)S(1)} %collective-permute-done.7.refs_2_) | copy-start | bytes 1572868
  88.2 12.5 %collective-permute-start.8 = (bf16[256,512]{1,0:T(8,128)(2,1)}, bf16[256,512]{1,0:T(8,128)(2,1)}, u32[]{:S(2)}, u32[]{:S(2)}) collective-permute-start(bf16[256,512]{1,0:T(8,128)(2,1)} %slice.47), channel_id=1, source_target_pairs={{0,3},{1,0},{2,1},{3,2},{4,7},{5,4},{6,5},{7,6},{8,11},{9,8},{10,9... | collective-permute-start | bytes 786440 | tf_op jit(solution)/shard_map/ppermute | solution.py:317
  100.8 3.3 %copy-start.9 = (bf16[256,512]{1,0:T(8,128)(2,1)}, bf16[256,512]{1,0:T(8,128)(2,1)S(1)}, u32[]{:S(2)}) copy-start(bf16[256,512]{1,0:T(8,128)(2,1)S(1)} %collective-permute-done.6.refs_3_) | copy-start | bytes 786436
  100.8 13.4 %collective-permute-start.11 = (bf16[512,512]{1,0:T(8,128)(2,1)S(1)}, bf16[512,512]{1,0:T(8,128)(2,1)S(1)}, u32[]{:S(2)}, u32[]{:S(2)}) collective-permute-start(bf16[512,512]{1,0:T(8,128)(2,1)S(1)} %get-tuple-element.55.refs_0_), channel_id=1, source_target_pairs={{0,1},{1,2},{2,3},{3,0},{4,5},{5,6},{6,7},{7,4},{8,9},{9,10},{10,1... | collective-permute-start | bytes 1572872 | tf_op jit(solution)/shard_map/ppermute | solution.py:317
  102.1 12.0 %collective-permute-start.12 = (bf16[512,512]{1,0:T(8,128)(2,1)S(1)}, bf16[512,512]{1,0:T(8,128)(2,1)S(1)}, u32[]{:S(2)}, u32[]{:S(2)}) collective-permute-start(bf16[512,512]{1,0:T(8,128)(2,1)S(1)} %get-tuple-element.55.refs_0_), channel_id=1, source_target_pairs={{0,3},{1,0},{2,1},{3,2},{4,7},{5,4},{6,5},{7,6},{8,11},{9,8},{10,9... | collective-permute-start | bytes 1572872 | tf_op jit(solution)/shard_map/ppermute | solution.py:317
  104.1 13.3 %copy-start.12 = (s32[1024]{0:T(1024)S(1)}, s32[1024]{0:T(1024)}, u32[]{:S(2)}) copy-start(s32[1024]{0:T(1024)} %param.12) | copy-start | bytes 12292
  104.1 13.3 %copy-start = (bf16[2048,2,512]{2,1,0:T(2,128)(2,1)S(1)}, bf16[2048,2,512]{2,1,0:T(2,128)(2,1)}, u32[]{:S(2)}) copy-start(bf16[2048,2,512]{2,1,0:T(2,128)(2,1)} %param.17) | copy-start | bytes 12582916
  114.2 16.2 %collective-permute-start.13 = (bf16[512,512]{1,0:T(8,128)(2,1)S(1)}, bf16[512,512]{1,0:T(8,128)(2,1)S(1)}, u32[]{:S(2)}, u32[]{:S(2)}) collective-permute-start(bf16[512,512]{1,0:T(8,128)(2,1)S(1)} %get-tuple-element.61.refs_0_), channel_id=1, source_target_pairs={{0,1},{1,2},{2,3},{3,0},{4,5},{5,6},{6,7},{7,4},{8,9},{9,10},{10,1... | collective-permute-start | bytes 1572872 | tf_op jit(solution)/shard_map/ppermute | solution.py:317
  115.0 15.4 %collective-permute-start.14 = (bf16[512,512]{1,0:T(8,128)(2,1)S(1)}, bf16[512,512]{1,0:T(8,128)(2,1)S(1)}, u32[]{:S(2)}, u32[]{:S(2)}) collective-permute-start(bf16[512,512]{1,0:T(8,128)(2,1)S(1)} %get-tuple-element.61.refs_0_), channel_id=1, source_target_pairs={{0,3},{1,0},{2,1},{3,2},{4,7},{5,4},{6,5},{7,6},{8,11},{9,8},{10,9... | collective-permute-start | bytes 1572872 | tf_op jit(solution)/shard_map/ppermute | solution.py:317
  127.0 9.2 %copy-start.2 = (bf16[512,512]{1,0:T(8,128)(2,1)S(1)}, bf16[512,512]{1,0:T(8,128)(2,1)}, u32[]{:S(2)}) copy-start(bf16[512,512]{1,0:T(8,128)(2,1)} %get-tuple-element.43.refs_0_.refs_9_) | copy-start | bytes 1572868
  127.0 9.2 %collective-permute-start.17 = (bf16[256,512]{1,0:T(8,128)(2,1)S(1)}, bf16[256,512]{1,0:T(8,128)(2,1)S(1)}, u32[]{:S(2)}, u32[]{:S(2)}) collective-permute-start(bf16[256,512]{1,0:T(8,128)(2,1)S(1)} %slice.42), channel_id=1, source_target_pairs={{0,1},{1,2},{2,3},{3,0},{4,5},{5,6},{6,7},{7,4},{8,9},{9,10},{10,1... | collective-permute-start | bytes 786440 | tf_op jit(solution)/shard_map/ppermute | solution.py:317
  127.1 9.1 %collective-permute-start.18 = (bf16[256,512]{1,0:T(8,128)(2,1)S(1)}, bf16[256,512]{1,0:T(8,128)(2,1)S(1)}, u32[]{:S(2)}, u32[]{:S(2)}) collective-permute-start(bf16[256,512]{1,0:T(8,128)(2,1)S(1)} %slice.43), channel_id=1, source_target_pairs={{0,3},{1,0},{2,1},{3,2},{4,7},{5,4},{6,5},{7,6},{8,11},{9,8},{10,9... | collective-permute-start | bytes 786440 | tf_op jit(solution)/shard_map/ppermute | solution.py:317
  130.4 8.6 %collective-permute-start.15 = (bf16[256,512]{1,0:T(8,128)(2,1)S(1)}, bf16[256,512]{1,0:T(8,128)(2,1)S(1)}, u32[]{:S(2)}, u32[]{:S(2)}) collective-permute-start(bf16[256,512]{1,0:T(8,128)(2,1)S(1)} %slice.40), channel_id=1, source_target_pairs={{0,1},{1,2},{2,3},{3,0},{4,5},{5,6},{6,7},{7,4},{8,9},{9,10},{10,1... | collective-permute-start | bytes 786440 | tf_op jit(solution)/shard_map/ppermute | solution.py:317
  130.5 8.4 %copy-start.1 = (bf16[512,512]{1,0:T(8,128)(2,1)S(1)}, bf16[512,512]{1,0:T(8,128)(2,1)}, u32[]{:S(2)}) copy-start(bf16[512,512]{1,0:T(8,128)(2,1)} %get-tuple-element.45.refs_0_.refs_9_) | copy-start | bytes 1572868
  130.5 8.4 %collective-permute-start.16 = (bf16[256,512]{1,0:T(8,128)(2,1)S(1)}, bf16[256,512]{1,0:T(8,128)(2,1)S(1)}, u32[]{:S(2)}, u32[]{:S(2)}) collective-permute-start(bf16[256,512]{1,0:T(8,128)(2,1)S(1)} %slice.41), channel_id=1, source_target_pairs={{0,3},{1,0},{2,1},{3,2},{4,7},{5,4},{6,5},{7,6},{8,11},{9,8},{10,9... | collective-permute-start | bytes 786440 | tf_op jit(solution)/shard_map/ppermute | solution.py:317

commit v2 on v1

--- a/solution.py
+++ b/solution.py
@@ -392,7 +392,10 @@
     context_left0, context_right0 = near(context0)
     context1, key1, value1 = layer(1, group, (later, left1, right1, *far1), *layer_args, [key0], [value0])
     context_left0, context_right0, context1 = lax.optimization_barrier((context_left0, context_right0, context1))
-    context_far0 = far(context_left0[:half], context_right0[half:])
+    context_left0_half, context_right0_half, value1 = lax.optimization_barrier(
+        (context_left0[:half], context_right0[half:], value1)
+    )
+    context_far0 = far(context_left0_half, context_right0_half)
     context_left1, context_right1 = near(context1)
     new_pool = write_pool(live_slot, cache_pool, [key0, key1], [value0, value1])
     context_left1, context_right1, new_pool = lax.optimization_barrier((context_left1, context_right1, new_pool))

time: 143 us -> 142 us (level)
  no operation moved by 1% of the time
where the time goes in v2:
time: 142 us; the launch traced here: 140 us
  starting transfers between devices  42.9 us (30%)
  Pallas kernels  40.4 us (28%)
  waiting for transfers between devices  40.2 us (28%)
  local copies, waits for them, and re-layouts  12 us (8%)
  other arithmetic  3.67 us (3%)
    ppermute x19, waiting for transfers between devices, shift(): lax.ppermute(values, 'tensor', [(i, (i + distance) % size) for i in range...  39.7 us
    ppermute x19, starting transfers between devices, shift(): lax.ppermute(values, 'tensor', [(i, (i + distance) % size) for i in range...  30.9 us
    pallas_call x2, Pallas kernels, layer(): pl.pallas_call(functools.partial(layer_kernel, number), grid_spec=pltpu.P...  17.8 us
    all_to_all x1, starting transfers between devices, shards(): got = lax.all_to_all(packed, 'req', split_axis=0, concat_axis=0, tiled=True)  12 us
    pallas_call x1, Pallas kernels, write_pool(): pl.pallas_call(pool_kernel, grid=(slots // step,), in_specs=[whole((1, ro...  9.49 us
    squeeze x1, local copies, waits for them, and re-layouts, shards(): weights = [projection[:, which, :] for which in range(3)]  5.71 us
    pallas_call x1, Pallas kernels, unpack(): pl.pallas_call(unpack_kernel, out_shape=[jax.ShapeDtypeStruct((chunk, wid...  4.7 us
    pallas_call x1, Pallas kernels, pack(): pl.pallas_call(functools.partial(pack_kernel, peers=peers), out_shape=jax...  4.3 us
  transfers between devices with their start and end apart: 20, of which 8 were waited for; matrix products, arithmetic and copies ran while one was open for 10% of the time, Pallas kernels for 21%

profile of v2, /device:TPU:2, one launch (start us, length us, event | category | flops | bytes accessed | tf_op | source)
XLA Modules:
  0.0 140.1 jit_solution(1300739216687326332)
XLA Ops:
  0.6 4.3 %pack.1 = bf16[64,72,128]{2,1,0:T(8,128)(2,1)} custom-call(s32[1,1024]{1,0:T(1,128)} %bitcast.27, bf16[1024,512]{1,0:T(8,128)(2,1)} %stream_ref.1), custom_call_target="tpu_custom_call" | custom-call | tf_op jit(solution)/shard_map/pack/pallas_call | solution.py:90
  4.9 12.0 %all-to-all-start = ((bf16[64,72,128]{2,1,0:T(8,128)(2,1)}), bf16[64,72,128]{2,1,0:T(8,128)(2,1)S(1)}, u32[]{:S(2)}, u32[]{:S(2)}) async-start(bf16[64,72,128]{2,1,0:T(8,128)(2,1)} %pack.1), calls=%async_computation | async-start | bytes 2359296 | tf_op jit(solution)/shard_map/all_to_all | solution.py:355
  17.0 0.0 copy-start.3
  17.0 1.7 %constant_dynamic-slice_fusion = (bf16[512,512]{1,0:T(8,128)(2,1)S(1)}, bf16[512,512]{1,0:T(8,128)(2,1)S(1)}, bf16[512,512]{1,0:T(8,128)(2,1)S(1)}, bf16[512,512]{1,0:T(8,128)(2,1)S(1)}) fusion(bf16[512,2048]{1,0:T(8,128)(2,1)} %param.16, s32[]{:T(128)S(6)} %select_n.59, s32[]{:T(128)S(6)} %select_n.58, s32[]{:T(128)S(6)} %select_n.57, s32[]{:T(128)S(6)} %select_n.56), kind=kLoop, calls=%fused_computation.18 | loop fusion | bytes 4194320 | tf_op jit(solution)/shard_map/dynamic_slice | solution.py:367
  18.7 1.7 %collective-permute-start = (bf16[512,512]{1,0:T(8,128)(2,1)S(1)}, bf16[512,512]{1,0:T(8,128)(2,1)S(1)}, u32[]{:S(2)}, u32[]{:S(2)}) collective-permute-start(bf16[512,512]{1,0:T(8,128)(2,1)S(1)} %get-tuple-element.85), channel_id=1, source_target_pairs={{0,1},{1,2},{2,3},{3,0},{4,5},{5,6},{6,7},{7,4},{8,9},{9,10},{10,1... | collective-permute-start | bytes 1572872 | tf_op jit(solution)/shard_map/ppermute | solution.py:317
  20.4 2.9 %collective-permute-start.1 = (bf16[512,512]{1,0:T(8,128)(2,1)S(1)}, bf16[512,512]{1,0:T(8,128)(2,1)S(1)}, u32[]{:S(2)}, u32[]{:S(2)}) collective-permute-start(bf16[512,512]{1,0:T(8,128)(2,1)S(1)} %get-tuple-element.84), channel_id=1, source_target_pairs={{0,2},{1,3},{2,0},{3,1},{4,6},{5,7},{6,4},{7,5},{8,10},{9,11},{10,... | collective-permute-start | bytes 1572872 | tf_op jit(solution)/shard_map/ppermute | solution.py:317
  23.3 1.3 collective-permute-start.2
  24.6 0.0 copy-done.3
  24.6 0.5 convert_reduce_fusion
  25.2 3.1 %fusion.3 = (f32[1024,128]{1,0:T(8,128)}, f32[1024,128]{1,0:T(8,128)}) fusion(f32[128]{0:T(128)S(1)} %get-tuple-element.89, f32[128]{0:T(128)S(1)} %get-tuple-element.90, f32[1024]{0:T(1024)S(1)} %convert_element_type.18, pred[128]{0:T(512)(128)(4,1)S(1)} %iota_compare_fusion.1), kind=kLoop, calls=%fused_computation.10 | loop fusion | flops 524288 | bytes 1053824 | tf_op jit(solution)/shard_map/jit(_where)/select_n | solution.py:331
  28.3 5.7 %slice_bitcast_fusion = (bf16[2048,512]{1,0:T(8,128)(2,1)}, bf16[2048,512]{1,0:T(8,128)(2,1)}, bf16[2048,512]{1,0:T(8,128)(2,1)}) fusion(bf16[2048,3,512]{2,0,1:T(8,128)(2,1)} %param.15), kind=kLoop, calls=%fused_computation.3 | loop fusion | bytes 12582912 | tf_op jit(solution)/shard_map/squeeze | solution.py:357
  34.0 0.0 collective-permute-done.refs_6_
  34.0 12.4 %collective-permute-done.1.refs_7_ = bf16[512,512]{1,0:T(8,128)(2,1)S(1)} collective-permute-done((bf16[512,512]{1,0:T(8,128)(2,1)S(1)}, bf16[512,512]{1,0:T(8,128)(2,1)S(1)}, u32[]{:S(2)}, u32[]{:S(2)}) %collective-permute-start.1) | collective-permute-done | bytes 524320 | tf_op jit(solution)/shard_map/ppermute | solution.py:317
  46.4 0.0 collective-permute-done.2.refs_8_
  46.5 0.5 all-to-all-done.got_ref
  47.0 1.0 copy-done.4
  48.0 4.7 %unpack.1 = (bf16[512,512]{1,0:T(8,128)(2,1)}, bf16[512,512]{1,0:T(8,128)(2,1)}) custom-call(bf16[64,72,128]{2,1,0:T(8,128)(2,1)} %copy-done.4), custom_call_target="tpu_custom_call" | custom-call | tf_op jit(solution)/shard_map/unpack/pallas_call | solution.py:120
  52.7 1.6 %collective-permute-start.3 = (bf16[512,512]{1,0:T(8,128)(2,1)}, bf16[512,512]{1,0:T(8,128)(2,1)S(1)}, u32[]{:S(2)}, u32[]{:S(2)}) collective-permute-start(bf16[512,512]{1,0:T(8,128)(2,1)} %get-tuple-element.46.refs_0_.refs_9_), channel_id=1, source_target_pairs={{0,1},{1,2},{2,3},{3,0},{4,5},{5,6},{6,7},{7,4},{8,9},{9,10},{10,1... | collective-permute-start | bytes 1572872 | tf_op jit(solution)/shard_map/ppermute | solution.py:317
  54.3 1.7 %collective-permute-start.4 = (bf16[512,512]{1,0:T(8,128)(2,1)}, bf16[512,512]{1,0:T(8,128)(2,1)S(1)}, u32[]{:S(2)}, u32[]{:S(2)}) collective-permute-start(bf16[512,512]{1,0:T(8,128)(2,1)} %get-tuple-element.46.refs_0_.refs_9_), channel_id=1, source_target_pairs={{0,3},{1,0},{2,1},{3,2},{4,7},{5,4},{6,5},{7,6},{8,11},{9,8},{10,9... | collective-permute-start | bytes 1572872 | tf_op jit(solution)/shard_map/ppermute | solution.py:317
  56.0 12.6 %collective-permute-done.3.refs_1_ = bf16[512,512]{1,0:T(8,128)(2,1)S(1)} collective-permute-done((bf16[512,512]{1,0:T(8,128)(2,1)}, bf16[512,512]{1,0:T(8,128)(2,1)S(1)}, u32[]{:S(2)}, u32[]{:S(2)}) %collective-permute-start.3) | collective-permute-done | bytes 524320 | tf_op jit(solution)/shard_map/ppermute | solution.py:317
  68.6 0.8 slice.44
  69.4 0.0 collective-permute-done.4.refs_2_
  69.4 0.8 slice.45
  70.1 0.0 copy-done.7
  70.1 0.2 copy-done.8
  70.3 1.4 %collective-permute-start.5 = (bf16[512,512]{1,0:T(8,128)(2,1)}, bf16[512,512]{1,0:T(8,128)(2,1)S(1)}, u32[]{:S(2)}, u32[]{:S(2)}) collective-permute-start(bf16[512,512]{1,0:T(8,128)(2,1)} %get-tuple-element.48.refs_0_.refs_9_), channel_id=1, source_target_pairs={{0,1},{1,2},{2,3},{3,0},{4,5},{5,6},{6,7},{7,4},{8,9},{9,10},{10,1... | collective-permute-start | bytes 1572872 | tf_op jit(solution)/shard_map/ppermute | solution.py:317
  71.7 1.8 %collective-permute-start.7 = (bf16[512,512]{1,0:T(8,128)(2,1)}, bf16[512,512]{1,0:T(8,128)(2,1)S(1)}, u32[]{:S(2)}, u32[]{:S(2)}) collective-permute-start(bf16[512,512]{1,0:T(8,128)(2,1)} %get-tuple-element.48.refs_0_.refs_9_), channel_id=1, source_target_pairs={{0,3},{1,0},{2,1},{3,2},{4,7},{5,4},{6,5},{7,6},{8,11},{9,8},{10,9... | collective-permute-start | bytes 1572872 | tf_op jit(solution)/shard_map/ppermute | solution.py:317
  73.5 1.5 %collective-permute-start.10 = (bf16[256,512]{1,0:T(8,128)(2,1)}, bf16[256,512]{1,0:T(8,128)(2,1)}, u32[]{:S(2)}, u32[]{:S(2)}) collective-permute-start(bf16[256,512]{1,0:T(8,128)(2,1)} %slice.45), channel_id=1, source_target_pairs={{0,3},{1,0},{2,1},{3,2},{4,7},{5,4},{6,5},{7,6},{8,11},{9,8},{10,9... | collective-permute-start | bytes 786440 | tf_op jit(solution)/shard_map/ppermute | solution.py:317
  75.0 0.6 collective-permute-start.9
  75.6 10.9 %collective-permute-done.5.refs_1_ = bf16[512,512]{1,0:T(8,128)(2,1)S(1)} collective-permute-done((bf16[512,512]{1,0:T(8,128)(2,1)}, bf16[512,512]{1,0:T(8,128)(2,1)S(1)}, u32[]{:S(2)}, u32[]{:S(2)}) %collective-permute-start.5) | collective-permute-done | bytes 524320 | tf_op jit(solution)/shard_map/ppermute | solution.py:317
  86.5 0.8 slice.46
  87.3 0.2 collective-permute-start.6
  87.5 0.0 collective-permute-done.7.refs_2_
  87.5 0.8 slice.47
  88.2 3.0 %collective-permute-start.8 = (bf16[256,512]{1,0:T(8,128)(2,1)}, bf16[256,512]{1,0:T(8,128)(2,1)}, u32[]{:S(2)}, u32[]{:S(2)}) collective-permute-start(bf16[256,512]{1,0:T(8,128)(2,1)} %slice.47), channel_id=1, source_target_pairs={{0,3},{1,0},{2,1},{3,2},{4,7},{5,4},{6,5},{7,6},{8,11},{9,8},{10,9... | collective-permute-start | bytes 786440 | tf_op jit(solution)/shard_map/ppermute | solution.py:317
  91.3 0.0 copy-done.10
  91.3 0.2 copy.20.refs_13_.refs_10_
  91.5 1.0 collective-permute-done.10.refs_4_
  92.5 0.0 collective-permute-done.9.refs_3_
  92.5 8.3 %layer.2 = (bf16[512,512]{1,0:T(8,128)(2,1)S(1)}, bf16[512,512]{1,0:T(8,128)(2,1)S(1)}, bf16[512,512]{1,0:T(8,128)(2,1)S(1)}) custom-call(s32[1]{0:T(128)} %bitcast.5.group_ref, bf16[512,512]{1,0:T(8,128)(2,1)} %get-tuple-element.46.refs_0_.refs_9_, bf16[512,512]{1,0:T(8,128)(2,1)} %copy-done.7, bf16[512,512]{1,0:T(8,128)(2,1)} %copy-done.8, ...), custom_call_target="tpu_custom_call" | custom-call | tf_op jit(solution)/shard_map/layer/pallas_call | solution.py:214
  100.8 0.0 collective-permute-done.6.refs_3_
  100.8 0.0 copy-start.9
  100.8 0.0 collective-permute-done.8.refs_4_
  100.8 1.4 collective-permute-start.11
  102.1 2.0 %collective-permute-start.12 = (bf16[512,512]{1,0:T(8,128)(2,1)S(1)}, bf16[512,512]{1,0:T(8,128)(2,1)S(1)}, u32[]{:S(2)}, u32[]{:S(2)}) collective-permute-start(bf16[512,512]{1,0:T(8,128)(2,1)S(1)} %get-tuple-element.58.refs_0_), channel_id=1, source_target_pairs={{0,3},{1,0},{2,1},{3,2},{4,7},{5,4},{6,5},{7,6},{8,11},{9,8},{10,9... | collective-permute-start | bytes 1572872 | tf_op jit(solution)/shard_map/ppermute | solution.py:317
  104.1 9.6 %layer.3 = (bf16[512,512]{1,0:T(8,128)(2,1)S(1)}, bf16[512,512]{1,0:T(8,128)(2,1)S(1)}, bf16[512,512]{1,0:T(8,128)(2,1)S(1)}) custom-call(s32[1]{0:T(128)} %bitcast.5.group_ref, bf16[512,512]{1,0:T(8,128)(2,1)} %get-tuple-element.48.refs_0_.refs_9_, bf16[512,512]{1,0:T(8,128)(2,1)} %copy-done.5, bf16[512,512]{1,0:T(8,128)(2,1)} %copy-done.6, ...), custom_call_target="tpu_custom_call" | custom-call | tf_op jit(solution)/shard_map/layer/pallas_call | solution.py:214
  113.7 0.5 collective-permute-done.11.refs_1_
  114.2 0.0 collective-permute-done.12.refs_2_
  114.2 0.8 collective-permute-start.13
  115.0 2.4 %collective-permute-start.14 = (bf16[512,512]{1,0:T(8,128)(2,1)S(1)}, bf16[512,512]{1,0:T(8,128)(2,1)S(1)}, u32[]{:S(2)}, u32[]{:S(2)}) collective-permute-start(bf16[512,512]{1,0:T(8,128)(2,1)S(1)} %get-tuple-element.64.refs_0_), channel_id=1, source_target_pairs={{0,3},{1,0},{2,1},{3,2},{4,7},{5,4},{6,5},{7,6},{8,11},{9,8},{10,9... | collective-permute-start | bytes 1572872 | tf_op jit(solution)/shard_map/ppermute | solution.py:317
  117.5 0.1 collective-permute-start.17
  117.6 3.2 %collective-permute-start.18 = (bf16[256,512]{1,0:T(8,128)(2,1)S(1)}, bf16[256,512]{1,0:T(8,128)(2,1)S(1)}, u32[]{:S(2)}, u32[]{:S(2)}) collective-permute-start(bf16[256,512]{1,0:T(8,128)(2,1)S(1)} %slice.41), channel_id=1, source_target_pairs={{0,3},{1,0},{2,1},{3,2},{4,7},{5,4},{6,5},{7,6},{8,11},{9,8},{10,9... | collective-permute-start | bytes 786440 | tf_op jit(solution)/shard_map/ppermute | solution.py:317
  120.8 9.5 %pool.1 = bf16[16384,128]{1,0:T(8,128)(2,1)} custom-call(s32[1,1024]{1,0:T(1,128)S(1)} %bitcast.25, bf16[16384,128]{1,0:T(8,128)(2,1)S(1)} %bitcast.21, bf16[512,512]{1,0:T(8,128)(2,1)S(1)} %get-tuple-element.61.refs_14_.refs_0_, bf16[512,512]{1,0:T(8,128)(2,1)S(1)} %get-tuple-element.66.refs_1_, bf16[512,512]{1,0:T(8,128)(2,1)S(1)} %get-tuple-element.62.refs_15_.refs_2_, ...), custom_call_target="tpu_custom_call" | custom-call | tf_op jit(solution)/shard_map/pool/pallas_call | solution.py:302
  130.3 0.0 collective-permute-done.13.refs_1_
  130.3 0.0 collective-permute-done.14.refs_2_
  130.3 1.2 collective-permute-start.15
  131.6 2.2 %collective-permute-start.16 = (bf16[256,512]{1,0:T(8,128)(2,1)S(1)}, bf16[256,512]{1,0:T(8,128)(2,1)S(1)}, u32[]{:S(2)}, u32[]{:S(2)}) collective-permute-start(bf16[256,512]{1,0:T(8,128)(2,1)S(1)} %slice.43), channel_id=1, source_target_pairs={{0,3},{1,0},{2,1},{3,2},{4,7},{5,4},{6,5},{7,6},{8,11},{9,8},{10,9... | collective-permute-start | bytes 786440 | tf_op jit(solution)/shard_map/ppermute | solution.py:317
  133.7 0.2 collective-permute-done.17.refs_3_
  133.9 0.0 collective-permute-done.18.refs_4_
  133.9 0.0 copy-done.2
  133.9 2.0 %finish.2.refs_11_ = bf16[1024,512]{1,0:T(8,128)(2,1)} custom-call(bf16[512,512]{1,0:T(8,128)(2,1)S(1)} %get-tuple-element.58.refs_0_, bf16[512,512]{1,0:T(8,128)(2,1)S(1)} %collective-permute-done.11.refs_1_, bf16[512,512]{1,0:T(8,128)(2,1)S(1)} %collective-permute-done.12.refs_2_, bf16[256,512]{1,0:T(8,128)(2,1)S(1)} %collective-permute-done.17.refs_3_, ...), custom_call_target="tpu_custom_call" | custom-call | tf_op jit(solution)/shard_map/finish/pallas_call | solution.py:256
  136.0 2.0 %collective-permute-done.15.refs_3_ = bf16[256,512]{1,0:T(8,128)(2,1)S(1)} collective-permute-done((bf16[256,512]{1,0:T(8,128)(2,1)S(1)}, bf16[256,512]{1,0:T(8,128)(2,1)S(1)}, u32[]{:S(2)}, u32[]{:S(2)}) %collective-permute-start.15) | collective-permute-done | bytes 262176 | tf_op jit(solution)/shard_map/ppermute | solution.py:317
  138.0 0.0 collective-permute-done.16.refs_4_
  138.0 2.0 %finish.3 = bf16[1024,512]{1,0:T(8,128)(2,1)} custom-call(bf16[512,512]{1,0:T(8,128)(2,1)S(1)} %get-tuple-element.64.refs_0_, bf16[512,512]{1,0:T(8,128)(2,1)S(1)} %collective-permute-done.13.refs_1_, bf16[512,512]{1,0:T(8,128)(2,1)S(1)} %collective-permute-done.14.refs_2_, ...), custom_call_target="tpu_custom_call", output_to_operand_aliasing={{}: (11, {})} | custom-call | tf_op jit(solution)/shard_map/finish/pallas_call | solution.py:256
  (28 shorter events, 0.1 us)
Async XLA Ops:
  4.9 42.0 %all-to-all-start = ((bf16[64,72,128]{2,1,0:T(8,128)(2,1)}), bf16[64,72,128]{2,1,0:T(8,128)(2,1)S(1)}, u32[]{:S(2)}, u32[]{:S(2)}) async-start(bf16[64,72,128]{2,1,0:T(8,128)(2,1)} %pack.1), calls=%async_computation | async-start | bytes 2359296 | tf_op jit(solution)/shard_map/all_to_all | solution.py:355
  17.0 7.6 %copy-start.3 = (s32[1024]{0:T(1024)S(1)}, s32[1024]{0:T(1024)}, u32[]{:S(2)}) copy-start(s32[1024]{0:T(1024)} %param.11) | copy-start | bytes 12292
  18.7 15.3 %collective-permute-start = (bf16[512,512]{1,0:T(8,128)(2,1)S(1)}, bf16[512,512]{1,0:T(8,128)(2,1)S(1)}, u32[]{:S(2)}, u32[]{:S(2)}) collective-permute-start(bf16[512,512]{1,0:T(8,128)(2,1)S(1)} %get-tuple-element.85), channel_id=1, source_target_pairs={{0,1},{1,2},{2,3},{3,0},{4,5},{5,6},{6,7},{7,4},{8,9},{9,10},{10,1... | collective-permute-start | bytes 1572872 | tf_op jit(solution)/shard_map/ppermute | solution.py:317
  20.4 26.1 %collective-permute-start.1 = (bf16[512,512]{1,0:T(8,128)(2,1)S(1)}, bf16[512,512]{1,0:T(8,128)(2,1)S(1)}, u32[]{:S(2)}, u32[]{:S(2)}) collective-permute-start(bf16[512,512]{1,0:T(8,128)(2,1)S(1)} %get-tuple-element.84), channel_id=1, source_target_pairs={{0,2},{1,3},{2,0},{3,1},{4,6},{5,7},{6,4},{7,5},{8,10},{9,11},{10,... | collective-permute-start | bytes 1572872 | tf_op jit(solution)/shard_map/ppermute | solution.py:317
  23.3 23.2 %collective-permute-start.2 = (bf16[512,512]{1,0:T(8,128)(2,1)S(1)}, bf16[512,512]{1,0:T(8,128)(2,1)S(1)}, u32[]{:S(2)}, u32[]{:S(2)}) collective-permute-start(bf16[512,512]{1,0:T(8,128)(2,1)S(1)} %get-tuple-element.83), channel_id=1, source_target_pairs={{0,3},{1,0},{2,1},{3,2},{4,7},{5,4},{6,5},{7,6},{8,11},{9,8},{10,9... | collective-permute-start | bytes 1572872 | tf_op jit(solution)/shard_map/ppermute | solution.py:317
  34.0 57.2 %copy-start.10 = (bf16[2048]{0:T(1024)(128)(2,1)S(1)}, bf16[2048]{0:T(1024)(128)(2,1)}, u32[]{:S(2)}) copy-start(bf16[2048]{0:T(1024)(128)(2,1)} %param.13) | copy-start | bytes 12292
  34.0 57.3 %copy-start.11 = (bf16[2048]{0:T(1024)(128)(2,1)S(1)}, bf16[2048]{0:T(1024)(128)(2,1)}, u32[]{:S(2)}) copy-start(bf16[2048]{0:T(1024)(128)(2,1)} %param.14) | copy-start | bytes 12292
  47.0 1.1 copy-start.4
  52.7 15.9 %collective-permute-start.3 = (bf16[512,512]{1,0:T(8,128)(2,1)}, bf16[512,512]{1,0:T(8,128)(2,1)S(1)}, u32[]{:S(2)}, u32[]{:S(2)}) collective-permute-start(bf16[512,512]{1,0:T(8,128)(2,1)} %get-tuple-element.46.refs_0_.refs_9_), channel_id=1, source_target_pairs={{0,1},{1,2},{2,3},{3,0},{4,5},{5,6},{6,7},{7,4},{8,9},{9,10},{10,1... | collective-permute-start | bytes 1572872 | tf_op jit(solution)/shard_map/ppermute | solution.py:317
  54.3 15.1 %collective-permute-start.4 = (bf16[512,512]{1,0:T(8,128)(2,1)}, bf16[512,512]{1,0:T(8,128)(2,1)S(1)}, u32[]{:S(2)}, u32[]{:S(2)}) collective-permute-start(bf16[512,512]{1,0:T(8,128)(2,1)} %get-tuple-element.46.refs_0_.refs_9_), channel_id=1, source_target_pairs={{0,3},{1,0},{2,1},{3,2},{4,7},{5,4},{6,5},{7,6},{8,11},{9,8},{10,9... | collective-permute-start | bytes 1572872 | tf_op jit(solution)/shard_map/ppermute | solution.py:317
  68.6 1.5 %copy-start.7 = (bf16[512,512]{1,0:T(8,128)(2,1)}, bf16[512,512]{1,0:T(8,128)(2,1)S(1)}, u32[]{:S(2)}) copy-start(bf16[512,512]{1,0:T(8,128)(2,1)S(1)} %collective-permute-done.3.refs_1_) | copy-start | bytes 1572868
  69.4 0.9 copy-start.8
  70.3 16.2 %collective-permute-start.5 = (bf16[512,512]{1,0:T(8,128)(2,1)}, bf16[512,512]{1,0:T(8,128)(2,1)S(1)}, u32[]{:S(2)}, u32[]{:S(2)}) collective-permute-start(bf16[512,512]{1,0:T(8,128)(2,1)} %get-tuple-element.48.refs_0_.refs_9_), channel_id=1, source_target_pairs={{0,1},{1,2},{2,3},{3,0},{4,5},{5,6},{6,7},{7,4},{8,9},{9,10},{10,1... | collective-permute-start | bytes 1572872 | tf_op jit(solution)/shard_map/ppermute | solution.py:317
  71.7 15.7 %collective-permute-start.7 = (bf16[512,512]{1,0:T(8,128)(2,1)}, bf16[512,512]{1,0:T(8,128)(2,1)S(1)}, u32[]{:S(2)}, u32[]{:S(2)}) collective-permute-start(bf16[512,512]{1,0:T(8,128)(2,1)} %get-tuple-element.48.refs_0_.refs_9_), channel_id=1, source_target_pairs={{0,3},{1,0},{2,1},{3,2},{4,7},{5,4},{6,5},{7,6},{8,11},{9,8},{10,9... | collective-permute-start | bytes 1572872 | tf_op jit(solution)/shard_map/ppermute | solution.py:317
  73.5 18.9 %collective-permute-start.10 = (bf16[256,512]{1,0:T(8,128)(2,1)}, bf16[256,512]{1,0:T(8,128)(2,1)}, u32[]{:S(2)}, u32[]{:S(2)}) collective-permute-start(bf16[256,512]{1,0:T(8,128)(2,1)} %slice.45), channel_id=1, source_target_pairs={{0,3},{1,0},{2,1},{3,2},{4,7},{5,4},{6,5},{7,6},{8,11},{9,8},{10,9... | collective-permute-start | bytes 786440 | tf_op jit(solution)/shard_map/ppermute | solution.py:317
  75.0 17.5 %collective-permute-start.9 = (bf16[256,512]{1,0:T(8,128)(2,1)}, bf16[256,512]{1,0:T(8,128)(2,1)}, u32[]{:S(2)}, u32[]{:S(2)}) collective-permute-start(bf16[256,512]{1,0:T(8,128)(2,1)} %slice.44), channel_id=1, source_target_pairs={{0,1},{1,2},{2,3},{3,0},{4,5},{5,6},{6,7},{7,4},{8,9},{9,10},{10,1... | collective-permute-start | bytes 786440 | tf_op jit(solution)/shard_map/ppermute | solution.py:317
  86.5 4.8 %copy-start.5 = (bf16[512,512]{1,0:T(8,128)(2,1)}, bf16[512,512]{1,0:T(8,128)(2,1)S(1)}, u32[]{:S(2)}) copy-start(bf16[512,512]{1,0:T(8,128)(2,1)S(1)} %collective-permute-done.5.refs_1_) | copy-start | bytes 1572868
  87.3 13.5 %collective-permute-start.6 = (bf16[256,512]{1,0:T(8,128)(2,1)}, bf16[256,512]{1,0:T(8,128)(2,1)S(1)}, u32[]{:S(2)}, u32[]{:S(2)}) collective-permute-start(bf16[256,512]{1,0:T(8,128)(2,1)} %slice.46), channel_id=1, source_target_pairs={{0,1},{1,2},{2,3},{3,0},{4,5},{5,6},{6,7},{7,4},{8,9},{9,10},{10,1... | collective-permute-start | bytes 786440 | tf_op jit(solution)/shard_map/ppermute | solution.py:317
  87.5 5.0 %copy-start.6 = (bf16[512,512]{1,0:T(8,128)(2,1)}, bf16[512,512]{1,0:T(8,128)(2,1)S(1)}, u32[]{:S(2)}) copy-start(bf16[512,512]{1,0:T(8,128)(2,1)S(1)} %collective-permute-done.7.refs_2_) | copy-start | bytes 1572868
  88.2 12.5 %collective-permute-start.8 = (bf16[256,512]{1,0:T(8,128)(2,1)}, bf16[256,512]{1,0:T(8,128)(2,1)}, u32[]{:S(2)}, u32[]{:S(2)}) collective-permute-start(bf16[256,512]{1,0:T(8,128)(2,1)} %slice.47), channel_id=1, source_target_pairs={{0,3},{1,0},{2,1},{3,2},{4,7},{5,4},{6,5},{7,6},{8,11},{9,8},{10,9... | collective-permute-start | bytes 786440 | tf_op jit(solution)/shard_map/ppermute | solution.py:317
  100.8 3.3 %copy-start.9 = (bf16[256,512]{1,0:T(8,128)(2,1)}, bf16[256,512]{1,0:T(8,128)(2,1)S(1)}, u32[]{:S(2)}) copy-start(bf16[256,512]{1,0:T(8,128)(2,1)S(1)} %collective-permute-done.6.refs_3_) | copy-start | bytes 786436
  100.8 13.4 %collective-permute-start.11 = (bf16[512,512]{1,0:T(8,128)(2,1)S(1)}, bf16[512,512]{1,0:T(8,128)(2,1)S(1)}, u32[]{:S(2)}, u32[]{:S(2)}) collective-permute-start(bf16[512,512]{1,0:T(8,128)(2,1)S(1)} %get-tuple-element.58.refs_0_), channel_id=1, source_target_pairs={{0,1},{1,2},{2,3},{3,0},{4,5},{5,6},{6,7},{7,4},{8,9},{9,10},{10,1... | collective-permute-start | bytes 1572872 | tf_op jit(solution)/shard_map/ppermute | solution.py:317
  102.1 12.0 %collective-permute-start.12 = (bf16[512,512]{1,0:T(8,128)(2,1)S(1)}, bf16[512,512]{1,0:T(8,128)(2,1)S(1)}, u32[]{:S(2)}, u32[]{:S(2)}) collective-permute-start(bf16[512,512]{1,0:T(8,128)(2,1)S(1)} %get-tuple-element.58.refs_0_), channel_id=1, source_target_pairs={{0,3},{1,0},{2,1},{3,2},{4,7},{5,4},{6,5},{7,6},{8,11},{9,8},{10,9... | collective-permute-start | bytes 1572872 | tf_op jit(solution)/shard_map/ppermute | solution.py:317
  104.1 13.3 %copy-start.12 = (s32[1024]{0:T(1024)S(1)}, s32[1024]{0:T(1024)}, u32[]{:S(2)}) copy-start(s32[1024]{0:T(1024)} %param.12) | copy-start | bytes 12292
  104.1 16.7 %copy-start = (bf16[2048,2,512]{2,1,0:T(2,128)(2,1)S(1)}, bf16[2048,2,512]{2,1,0:T(2,128)(2,1)}, u32[]{:S(2)}) copy-start(bf16[2048,2,512]{2,1,0:T(2,128)(2,1)} %param.17) | copy-start | bytes 12582916
  114.2 16.1 %collective-permute-start.13 = (bf16[512,512]{1,0:T(8,128)(2,1)S(1)}, bf16[512,512]{1,0:T(8,128)(2,1)S(1)}, u32[]{:S(2)}, u32[]{:S(2)}) collective-permute-start(bf16[512,512]{1,0:T(8,128)(2,1)S(1)} %get-tuple-element.64.refs_0_), channel_id=1, source_target_pairs={{0,1},{1,2},{2,3},{3,0},{4,5},{5,6},{6,7},{7,4},{8,9},{9,10},{10,1... | collective-permute-start | bytes 1572872 | tf_op jit(solution)/shard_map/ppermute | solution.py:317
  115.0 15.3 %collective-permute-start.14 = (bf16[512,512]{1,0:T(8,128)(2,1)S(1)}, bf16[512,512]{1,0:T(8,128)(2,1)S(1)}, u32[]{:S(2)}, u32[]{:S(2)}) collective-permute-start(bf16[512,512]{1,0:T(8,128)(2,1)S(1)} %get-tuple-element.64.refs_0_), channel_id=1, source_target_pairs={{0,3},{1,0},{2,1},{3,2},{4,7},{5,4},{6,5},{7,6},{8,11},{9,8},{10,9... | collective-permute-start | bytes 1572872 | tf_op jit(solution)/shard_map/ppermute | solution.py:317
  117.5 16.4 %collective-permute-start.17 = (bf16[256,512]{1,0:T(8,128)(2,1)S(1)}, bf16[256,512]{1,0:T(8,128)(2,1)S(1)}, u32[]{:S(2)}, u32[]{:S(2)}) collective-permute-start(bf16[256,512]{1,0:T(8,128)(2,1)S(1)} %slice.40), channel_id=1, source_target_pairs={{0,1},{1,2},{2,3},{3,0},{4,5},{5,6},{6,7},{7,4},{8,9},{9,10},{10,1... | collective-permute-start | bytes 786440 | tf_op jit(solution)/shard_map/ppermute | solution.py:317
  117.6 16.4 %collective-permute-start.18 = (bf16[256,512]{1,0:T(8,128)(2,1)S(1)}, bf16[256,512]{1,0:T(8,128)(2,1)S(1)}, u32[]{:S(2)}, u32[]{:S(2)}) collective-permute-start(bf16[256,512]{1,0:T(8,128)(2,1)S(1)} %slice.41), channel_id=1, source_target_pairs={{0,3},{1,0},{2,1},{3,2},{4,7},{5,4},{6,5},{7,6},{8,11},{9,8},{10,9... | collective-permute-start | bytes 786440 | tf_op jit(solution)/shard_map/ppermute | solution.py:317
  120.8 13.1 %copy-start.2 = (bf16[512,512]{1,0:T(8,128)(2,1)S(1)}, bf16[512,512]{1,0:T(8,128)(2,1)}, u32[]{:S(2)}) copy-start(bf16[512,512]{1,0:T(8,128)(2,1)} %get-tuple-element.46.refs_0_.refs_9_) | copy-start | bytes 1572868
  130.3 7.7 %collective-permute-start.15 = (bf16[256,512]{1,0:T(8,128)(2,1)S(1)}, bf16[256,512]{1,0:T(8,128)(2,1)S(1)}, u32[]{:S(2)}, u32[]{:S(2)}) collective-permute-start(bf16[256,512]{1,0:T(8,128)(2,1)S(1)} %slice.42), channel_id=1, source_target_pairs={{0,1},{1,2},{2,3},{3,0},{4,5},{5,6},{6,7},{7,4},{8,9},{9,10},{10,1... | collective-permute-start | bytes 786440 | tf_op jit(solution)/shard_map/ppermute | solution.py:317
  131.6 6.5 %copy-start.1 = (bf16[512,512]{1,0:T(8,128)(2,1)S(1)}, bf16[512,512]{1,0:T(8,128)(2,1)}, u32[]{:S(2)}) copy-start(bf16[512,512]{1,0:T(8,128)(2,1)} %get-tuple-element.48.refs_0_.refs_9_) | copy-start | bytes 1572868
  131.6 6.4 %collective-permute-start.16 = (bf16[256,512]{1,0:T(8,128)(2,1)S(1)}, bf16[256,512]{1,0:T(8,128)(2,1)S(1)}, u32[]{:S(2)}, u32[]{:S(2)}) collective-permute-start(bf16[256,512]{1,0:T(8,128)(2,1)S(1)} %slice.43), channel_id=1, source_target_pairs={{0,3},{1,0},{2,1},{3,2},{4,7},{5,4},{6,5},{7,6},{8,11},{9,8},{10,9... | collective-permute-start | bytes 786440 | tf_op jit(solution)/shard_map/ppermute | solution.py:317
